TPU v7x, 32 devices: a whole 2x2x4 slice. The times are simulated.
32 devices in a mesh: dp: 8 (over z, x), row: 4 (over y, core).
Axes of the slice: x: 2, y: 2, z: 4, core: 2. Of those that a mesh axis runs over, the one named last changes fastest.
Arguments:
- queries: bfloat16 [2048, 4096], P('dp', 'row'), may hold values from -100 to 100
- passages: bfloat16 [2048, 4096], P('dp', 'row'), may hold values from -10 to 10
- cached: bfloat16 [16384, 4096], P('dp', 'row'), may hold values from -6 to 6
- hard_shard: int32 [2048, 4], P('dp'), may hold values from 0 to 7, as said below
- hard_row: int32 [2048, 4], P('dp'), may hold values from 0 to 2047
- query_source: int32 [2048], P('dp'), may hold values from 0 to 7
- block_source: int32 [16], replicated, may hold values from 0 to 7
Outputs:
- mean_loss: float32 [], replicated
- query_grad: bfloat16 [2048, 4096], P('dp', 'row')
- passage_grad: bfloat16 [2048, 4096], P('dp', 'row')
Inputs may be any that keep to these rules, and one draw needn't show every extreme that they name: `hard_shard`: one cache shard, drawn with the seed, is named exactly 256 times among the 256 queries of every device; among one device's queries no shard is named more than 256 times, and the other shards share the rest as evenly as possible; a query's 4 hard negatives lie in 4 different shards.
All inputs are finite; a program needn't handle non-finite values.
Results may differ from a plain program's by a relative error of at most 0.0043.
Values may be sent and summed in bfloat16 or wider, within the bound.
A program may use at most 128 MiB of HBM per device.

v0:
```python
import functools
import math

import jax
import jax.numpy as jnp
from jax import lax
from jax.experimental import pallas as pl
from jax.experimental.pallas import tpu as pltpu
from jax.sharding import PartitionSpec as P

D = 4096
BLOCK = 128
LANES = 128
NEG_FILL = -1e30
MESH = pl.DeviceIdType.MESH


def spill_kernel(n, hot, rows_ref, out, send, recv, own_sem):
    me = lax.axis_index("dp")
    r = lax.axis_index("row")
    barrier = pltpu.get_barrier_semaphore()

    def copy(j):
        to = (hot + j) % n
        return pltpu.make_async_remote_copy(
            src_ref=rows_ref.at[to],
            dst_ref=out,
            send_sem=send.at[j - 1],
            recv_sem=recv,
            device_id=(to, r),
            device_id_type=MESH,
        )

    @pl.when(me == hot)
    def _():
        for j in range(1, n):
            pl.semaphore_signal(
                barrier, inc=1, device_id=((hot + j) % n, r), device_id_type=MESH
            )

    @pl.when(me != hot)
    def _():
        pl.semaphore_signal(barrier, inc=1, device_id=(hot, r), device_id_type=MESH)

    pl.semaphore_wait(barrier, 1 + (me == hot).astype(jnp.int32) * (n - 2))

    @pl.when(me == hot)
    def _():
        for j in range(1, n):
            copy(j).start()
        own = pltpu.make_async_copy(rows_ref.at[hot], out, own_sem)
        own.start()
        own.wait()
        for j in range(1, n):
            copy(j).wait_send()

    @pl.when(me != hot)
    def _():
        copy(1).wait_recv()


def spill(n, hot, rows):
    vmem = pl.BlockSpec(memory_space=pltpu.VMEM)
    dma = pltpu.SemaphoreType.DMA
    return pl.pallas_call(
        functools.partial(spill_kernel, n, hot),
        name=f"spill_{hot}",
        out_shape=jax.ShapeDtypeStruct(rows.shape[1:], rows.dtype),
        in_specs=[vmem],
        out_specs=vmem,
        scratch_shapes=[dma((n - 1,)), dma(()), dma(())],
        compiler_params=pltpu.CompilerParams(collective_id=3 + hot, has_side_effects=True),
    )(rows)


def fetch_hard(cached, hard_shard, hard_row, n_data):
    row_count, hard_count = hard_shard.shape
    width_dev = cached.shape[1]
    capacity = min(row_count, 3 * row_count * hard_count // n_data)
    others = -(-(row_count * hard_count - capacity) // (n_data - 1))
    common = min(capacity - 16, -(-others // 16) * 16)
    owners = hard_shard.reshape(-1)
    wanted = hard_row.reshape(-1)
    one_hot = (owners[:, None] == jnp.arange(n_data, dtype=jnp.int32)[None, :]).astype(jnp.int32)
    before = jnp.cumsum(one_hot, axis=0) - one_hot
    slot_index = jnp.sum(before * one_hot, axis=1)
    hot = jnp.argmax(jnp.sum(one_hot, axis=0)).astype(jnp.int32)
    target = owners * capacity + slot_index
    requests = (
        jnp.zeros((n_data * capacity,), jnp.int32).at[target].set(wanted).reshape(n_data, capacity)
    )
    asked_rows = lax.all_to_all(requests, "dp", split_axis=0, concat_axis=0, tiled=True)
    picked = jnp.take(cached, asked_rows[:, :common].reshape(-1), axis=0, mode="clip")
    picked = picked.reshape(n_data, common, width_dev)
    replies = lax.all_to_all(picked, "dp", split_axis=0, concat_axis=0, tiled=True)
    extra = jnp.take(cached, asked_rows[:, common:].reshape(-1), axis=0, mode="clip")
    extra = extra.reshape(n_data, capacity - common, width_dev)
    spilled = lax.switch(hot, [functools.partial(spill, n_data, k) for k in range(n_data)], extra)
    reply_rows = jnp.concatenate([replies.reshape(n_data * common, width_dev), spilled], axis=0)
    place = jnp.where(
        slot_index < common, owners * common + slot_index, n_data * common + slot_index - common
    )
    by_slot = place.reshape(row_count, hard_count).T.reshape(-1)
    hard_rows = jnp.take(reply_rows, by_slot, axis=0, mode="clip")
    return hard_rows.reshape(hard_count, row_count, width_dev)


def gather_kernel(n, n_row, q_ref, p_ref, pall, qall, lsum, lpart, lrecv,
                  gsend, grecv, lsend, lrecv_sem, own_sem):
    me = lax.axis_index("dp")
    r = lax.axis_index("row")
    lines = n // 2
    a = me // 2
    b = me % 2
    rows = q_ref.shape[0]
    part = rows // n_row
    across = a * 2 + 1 - b

    barrier = pltpu.get_barrier_semaphore()
    pl.semaphore_signal(barrier, inc=1, device_id=(across, r), device_id_type=MESH)
    for k in range(1, n_row):
        pl.semaphore_signal(
            barrier, inc=1, device_id=(me, lax.rem(r + k, n_row)), device_id_type=MESH
        )

    @pl.when(a < lines - 1)
    def _():
        pl.semaphore_signal(barrier, inc=1, device_id=(me + 2, r), device_id_type=MESH)

    @pl.when(a > 0)
    def _():
        pl.semaphore_signal(barrier, inc=1, device_id=(me - 2, r), device_id_type=MESH)

    neighbours = (a < lines - 1).astype(jnp.int32) + (a > 0).astype(jnp.int32)
    pl.semaphore_wait(barrier, n_row + neighbours)

    alls = (pall, qall)
    own = (p_ref, q_ref)

    def copy(t, kind, blk, first=False):
        to = (across, me + 2, me - 2)[kind]
        return pltpu.make_async_remote_copy(
            src_ref=own[t] if first else alls[t].at[blk],
            dst_ref=alls[t].at[blk],
            send_sem=gsend.at[t, kind, blk],
            recv_sem=grecv.at[t, blk],
            device_id=(to, r),
            device_id_type=MESH,
        )

    def arrived(t, blk):
        copy(t, 0, blk).wait_recv()

    def start_own(t):
        @pl.when(a < lines - 1)
        def _():
            copy(t, 1, me, True).start()

        @pl.when(a > 0)
        def _():
            copy(t, 2, me, True).start()

        copy(t, 0, me, True).start()

    def multiply(blk, block):
        lpart[blk] = lax.dot_general(
            q_ref[...], block, (((1,), (1,)), ((), ())), preferred_element_type=jnp.float32
        )

    def ship(blk):
        for k in range(1, n_row):
            to = lax.rem(r + k, n_row)
            ship_copy(blk, to, k).start()

    def ship_copy(blk, to, k):
        return pltpu.make_async_remote_copy(
            src_ref=lpart.at[blk, pl.ds(pl.multiple_of(to * part, part), part), :],
            dst_ref=lrecv.at[k - 1, blk],
            send_sem=lsend.at[k - 1, blk],
            recv_sem=lrecv_sem.at[k - 1, blk],
            device_id=(me, to),
            device_id_type=MESH,
        )

    def relay(t, s):
        lo = me - 2 * (s + 1)
        hi = me + 2 * (s + 1)

        @pl.when(lo >= 0)
        def _():
            arrived(t, lo)

            @pl.when(a < lines - 1)
            def _():
                copy(t, 1, lo).start()

            copy(t, 0, lo).start()

        @pl.when(hi < n)
        def _():
            arrived(t, hi)

            @pl.when(a > 0)
            def _():
                copy(t, 2, hi).start()

            copy(t, 0, hi).start()

    def logits_of(s):
        lo = me - 2 * (s + 1)
        hi = me + 2 * (s + 1)
        flip = 1 - 2 * b

        @pl.when(lo >= 0)
        def _():
            multiply(lo, pall[lo])

        @pl.when(hi < n)
        def _():
            multiply(hi, pall[hi])

        @pl.when(lo >= 0)
        def _():
            ship(lo)
            arrived(0, lo + flip)
            multiply(lo + flip, pall[lo + flip])

        @pl.when(hi < n)
        def _():
            ship(hi)
            arrived(0, hi + flip)
            multiply(hi + flip, pall[hi + flip])

        @pl.when(lo >= 0)
        def _():
            ship(lo + flip)

        @pl.when(hi < n)
        def _():
            ship(hi + flip)

    start_own(0)
    own_p = pltpu.make_async_copy(p_ref, pall.at[me], own_sem.at[0])
    own_q = pltpu.make_async_copy(q_ref, qall.at[me], own_sem.at[1])
    own_p.start()
    own_q.start()
    multiply(me, p_ref[...])
    for s in range(lines - 1):
        relay(0, s)
        if s == lines - 2:
            start_own(1)
        if s == 0:
            ship(me)
            arrived(0, across)
            multiply(across, pall[across])
            ship(across)
        else:
            logits_of(s - 1)
    for s in range(lines - 1):
        relay(1, s)
        if s == 0:
            logits_of(lines - 2)
    arrived(1, across)
    flip = 1 - 2 * b
    for s in range(lines - 1):
        lo = me - 2 * (s + 1)
        hi = me + 2 * (s + 1)

        @pl.when(lo >= 0)
        def _():
            arrived(1, lo + flip)

        @pl.when(hi < n)
        def _():
            arrived(1, hi + flip)

    base = pl.multiple_of(r * part, part)
    columns = p_ref.shape[0]
    for blk in range(n):
        total = lpart[blk, pl.ds(base, part), :]
        for k in range(1, n_row):
            ship_copy(blk, lax.rem(r + k, n_row), k).wait_recv()
            total = total + lrecv[k - 1, blk]
        lsum[:, blk * columns:(blk + 1) * columns] = total

    own_p.wait()
    own_q.wait()
    for blk in range(n):
        for k in range(1, n_row):
            ship_copy(blk, lax.rem(r + k, n_row), k).wait_send()
    for t in range(2):
        copy(t, 0, me, True).wait_send()

        @pl.when(a < lines - 1)
        def _():
            copy(t, 1, me, True).wait_send()

        @pl.when(a > 0)
        def _():
            copy(t, 2, me, True).wait_send()

        for s in range(lines - 1):
            lo = me - 2 * (s + 1)
            hi = me + 2 * (s + 1)

            @pl.when(lo >= 0)
            def _():
                copy(t, 0, lo).wait_send()

                @pl.when(a < lines - 1)
                def _():
                    copy(t, 1, lo).wait_send()

            @pl.when(hi < n)
            def _():
                copy(t, 0, hi).wait_send()

                @pl.when(a > 0)
                def _():
                    copy(t, 2, hi).wait_send()


def gather_and_logits(queries, passages, n, n_row):
    rows, width = queries.shape
    prows = passages.shape[0]
    part = rows // n_row
    vmem = pl.BlockSpec(memory_space=pltpu.VMEM)
    return pl.pallas_call(
        functools.partial(gather_kernel, n, n_row),
        name="gather_logits",
        out_shape=(
            jax.ShapeDtypeStruct((n, prows, width), passages.dtype),
            jax.ShapeDtypeStruct((n, rows, width), queries.dtype),
            jax.ShapeDtypeStruct((part, n * prows), jnp.float32),
        ),
        in_specs=[vmem, vmem],
        out_specs=(vmem, vmem, vmem),
        scratch_shapes=[
            pltpu.VMEM((n, rows, prows), jnp.float32),
            pltpu.VMEM((n_row - 1, n, part, prows), jnp.float32),
            pltpu.SemaphoreType.DMA((2, 3, n)),
            pltpu.SemaphoreType.DMA((2, n)),
            pltpu.SemaphoreType.DMA((n_row - 1, n)),
            pltpu.SemaphoreType.DMA((n_row - 1, n)),
            pltpu.SemaphoreType.DMA((2,)),
        ],
        compiler_params=pltpu.CompilerParams(
            collective_id=0, has_side_effects=True, vmem_limit_bytes=56 * 2**20
        ),
    )(queries, passages)


def weights_kernel(n, n_row, columns, w_ref, loss_ref, wrow, wcol, table, dsend, drecv, tsend,
                   trecv, rsend, rrecv, own_sem):
    me = lax.axis_index("dp")
    r = lax.axis_index("row")
    n_line = n_row // 2
    y = r // 2
    core = r % 2
    partner = y * 2 + 1 - core
    barrier = pltpu.get_barrier_semaphore()
    for j in range(1, n):
        pl.semaphore_signal(
            barrier, inc=1, device_id=(lax.rem(me + j, n), r), device_id_type=MESH
        )
    for k in range(1, n_line):
        pl.semaphore_signal(
            barrier, inc=1, device_id=(me, lax.rem(r + 2 * k, n_row)), device_id_type=MESH
        )
    pl.semaphore_signal(barrier, inc=1, device_id=(me, partner), device_id_type=MESH)
    pl.semaphore_wait(barrier, n + n_line - 1)

    def across(j):
        to = lax.rem(me + j, n)
        return pltpu.make_async_remote_copy(
            src_ref=w_ref.at[:, pl.ds(pl.multiple_of(to * columns, columns), columns)],
            dst_ref=wcol.at[y, core, me],
            send_sem=dsend.at[j - 1],
            recv_sem=drecv.at[j - 1],
            device_id=(to, r),
            device_id_type=MESH,
        )

    def tell(j):
        return pltpu.make_async_remote_copy(
            src_ref=loss_ref,
            dst_ref=table.at[y, core, me],
            send_sem=tsend.at[j - 1],
            recv_sem=trecv.at[j - 1],
            device_id=(lax.rem(me + j, n), r),
            device_id_type=MESH,
        )

    def along(which, k):
        out = (wrow, wcol, table)[which]
        return pltpu.make_async_remote_copy(
            src_ref=w_ref if which == 0 else out.at[y, core],
            dst_ref=out.at[y, core],
            send_sem=rsend.at[which, k - 1],
            recv_sem=rrecv.at[which, k - 1],
            device_id=(me, lax.rem(r + 2 * k, n_row)),
            device_id_type=MESH,
        )

    def beside(which):
        out = (wrow, wcol, table)[which]
        return pltpu.make_async_remote_copy(
            src_ref=out.at[:, core],
            dst_ref=out.at[:, core],
            send_sem=rsend.at[which, n_line - 1],
            recv_sem=rrecv.at[which, n_line - 1],
            device_id=(me, partner),
            device_id_type=MESH,
        )

    for j in range(1, n):
        across(j).start()
        tell(j).start()
    for k in range(1, n_line):
        along(0, k).start()
    owns = (
        pltpu.make_async_copy(w_ref, wrow.at[y, core], own_sem.at[0]),
        pltpu.make_async_copy(
            w_ref.at[:, pl.ds(pl.multiple_of(me * columns, columns), columns)],
            wcol.at[y, core, me],
            own_sem.at[1],
        ),
        pltpu.make_async_copy(loss_ref, table.at[y, core, me], own_sem.at[2]),
    )
    for own in owns:
        own.start()
    for own in owns:
        own.wait()
    for j in range(1, n):
        across(j).wait_recv()
        tell(j).wait_recv()
    for k in range(1, n_line):
        along(1, k).start()
        along(2, k).start()
    for which in range(3):
        for k in range(1, n_line):
            along(which, k).wait_recv()
        beside(which).start()
    for which in range(3):
        beside(which).wait_recv()
    for j in range(1, n):
        across(j).wait_send()
        tell(j).wait_send()
    for which in range(3):
        for k in range(1, n_line):
            along(which, k).wait_send()
        beside(which).wait_send()


def exchange_weights(weights_ext, loss_tile, n, n_row, columns):
    part, wide = weights_ext.shape
    vmem = pl.BlockSpec(memory_space=pltpu.VMEM)
    dma = pltpu.SemaphoreType.DMA
    n_line = n_row // 2
    return pl.pallas_call(
        functools.partial(weights_kernel, n, n_row, columns),
        name="exchange_weights",
        out_shape=(
            jax.ShapeDtypeStruct((n_line, 2, part, wide), weights_ext.dtype),
            jax.ShapeDtypeStruct((n_line, 2, n, part, columns), weights_ext.dtype),
            jax.ShapeDtypeStruct((n_line, 2, n) + loss_tile.shape, loss_tile.dtype),
        ),
        in_specs=[vmem, vmem],
        out_specs=(vmem, vmem, vmem),
        scratch_shapes=[
            dma((n - 1,)), dma((n - 1,)), dma((n - 1,)), dma((n - 1,)),
            dma((3, n_line)), dma((3, n_line)), dma((3,)),
        ],
        compiler_params=pltpu.CompilerParams(collective_id=1, has_side_effects=True),
    )(weights_ext, loss_tile)


def hard_kernel(n_row, x_ref, out, send, recv, own_sem):
    me = lax.axis_index("dp")
    r = lax.axis_index("row")
    barrier = pltpu.get_barrier_semaphore()
    for k in range(1, n_row):
        pl.semaphore_signal(
            barrier, inc=1, device_id=(me, lax.rem(r + k, n_row)), device_id_type=MESH
        )
    pl.semaphore_wait(barrier, n_row - 1)

    def along(k):
        return pltpu.make_async_remote_copy(
            src_ref=x_ref,
            dst_ref=out.at[r],
            send_sem=send.at[k - 1],
            recv_sem=recv.at[k - 1],
            device_id=(me, lax.rem(r + k, n_row)),
            device_id_type=MESH,
        )

    for k in range(1, n_row):
        along(k).start()
    own = pltpu.make_async_copy(x_ref, out.at[r], own_sem)
    own.start()
    own.wait()
    for k in range(1, n_row):
        along(k).wait()


def gather_hard(partial_hard, n_row):
    vmem = pl.BlockSpec(memory_space=pltpu.VMEM)
    dma = pltpu.SemaphoreType.DMA
    return pl.pallas_call(
        functools.partial(hard_kernel, n_row),
        name="gather_hard",
        out_shape=jax.ShapeDtypeStruct((n_row,) + partial_hard.shape, partial_hard.dtype),
        in_specs=[vmem],
        out_specs=vmem,
        scratch_shapes=[dma((n_row - 1,)), dma((n_row - 1,)), dma(())],
        compiler_params=pltpu.CompilerParams(collective_id=2, has_side_effects=True),
    )(partial_hard)


def softmax_rows(summed, summed_hard, sources, block_source, first_row, logit_scale):
    logits = logit_scale * summed
    hard_logits = logit_scale * summed_hard
    columns = jnp.arange(logits.shape[1], dtype=jnp.int32)
    targets = first_row + jnp.arange(logits.shape[0], dtype=jnp.int32)
    column_source = jnp.repeat(block_source, BLOCK)
    positive = columns[None, :] == targets[:, None]
    allowed = (sources[:, None] != column_source[None, :]) | positive
    masked = jnp.where(allowed, logits, NEG_FILL)
    maximum = jnp.maximum(jnp.max(masked, axis=1), jnp.max(hard_logits, axis=1))
    exponent = jnp.exp(masked - maximum[:, None])
    hard_expo = jnp.exp(hard_logits - maximum[:, None])
    totals = jnp.sum(exponent, axis=1) + jnp.sum(hard_expo, axis=1)
    pos_logit = jnp.sum(jnp.where(positive, logits, 0.0), axis=1)
    per_query = maximum + jnp.log(totals) - pos_logit
    weights = (exponent / totals[:, None] - positive.astype(jnp.float32)).astype(jnp.bfloat16)
    hard_weights = (hard_expo / totals[:, None]).astype(jnp.bfloat16)
    return (weights, hard_weights, jnp.sum(per_query))


def on_device(queries, passages, cached, hard_shard, hard_row, query_source, block_source):
    row_count, width = queries.shape
    columns = passages.shape[0]
    n_data = lax.axis_size("dp")
    n_row = lax.axis_size("row")
    part = row_count // n_row
    logit_scale = 1.0 / math.sqrt(D)
    hard_rows = fetch_hard(cached, hard_shard, hard_row, n_data)
    hard_count = hard_rows.shape[0]
    pall, qall, summed = gather_and_logits(queries, passages, n_data, n_row)
    partial_hard = jnp.sum(
        queries.astype(jnp.float32)[None] * hard_rows.astype(jnp.float32), axis=2
    )
    partial_hard = jnp.pad(partial_hard, ((0, -hard_count % 8), (0, 0)))
    summed_hard = jnp.sum(gather_hard(partial_hard, n_row), axis=0)[:hard_count]
    row_at = lax.axis_index("row") * part
    first_row = lax.axis_index("dp") * row_count + row_at
    my_hard = lax.dynamic_slice_in_dim(summed_hard, row_at, part, 1).T
    my_source = lax.dynamic_slice_in_dim(query_source, row_at, part, 0)
    weights, hard_weights, local_loss = softmax_rows(
        summed, my_hard, my_source, block_source, first_row, logit_scale
    )
    n_all = weights.shape[1]
    ext = jnp.concatenate(
        [weights, jnp.pad(hard_weights, ((0, 0), (0, LANES - hard_count)))], axis=1
    )
    loss_tile = jnp.full((8, LANES), local_loss, jnp.float32)
    wrow, wcol, losses = exchange_weights(ext, loss_tile, n_data, n_row, columns)
    loss_sum = jnp.sum(losses[:, :, :, 0, 0])
    mean_loss = loss_sum / (row_count * n_data)
    wrow = wrow.reshape(row_count, n_all + LANES)
    query_grad = jnp.dot(
        wrow[:, :n_all], pall.reshape(n_data * columns, width), preferred_element_type=jnp.float32
    )
    for h in range(hard_count):
        query_grad = query_grad + wrow[:, n_all + h:n_all + h + 1].astype(
            jnp.float32
        ) * hard_rows[h].astype(jnp.float32)
    passage_grad = lax.dot_general(
        wcol.reshape(n_row, n_data, part, columns),
        qall.reshape(n_data, n_row, part, width).transpose(1, 0, 2, 3),
        (((0, 1, 2), (0, 1, 2)), ((), ())),
        preferred_element_type=jnp.float32,
    )
    return (mean_loss, query_grad.astype(jnp.bfloat16), passage_grad.astype(jnp.bfloat16))


def solution(mesh):
    in_specs = (
        P("dp", "row"),
        P("dp", "row"),
        P("dp", "row"),
        P("dp", None),
        P("dp", None),
        P("dp"),
        P(),
    )
    out_specs = (P(), P("dp", "row"), P("dp", "row"))
    return jax.shard_map(
        on_device, mesh=mesh, in_specs=in_specs, out_specs=out_specs, check_vma=False
    )
```

profile of v0, /device:TPU:0, one launch (start us, length us, event | category | flops | bytes accessed | tf_op | source)
XLA Modules:
  0.0 269.3 jit_solution(7690380639143112805)
XLA Ops:
  0.6 0.8 copy.35
  2.4 2.3 reduce-window.6
  5.5 0.8 copy.37
  6.6 4.3 %scatter_custom_fusion = s32[2048]{0:T(1024)S(1)} fusion(s32[1024]{0:T(1024)S(1)} %bitcast.71, s32[1024]{0:T(1024)S(1)} %reshape.192, s32[]{:T(128)} %constant.19.clone.1), kind=kCustom, calls=%fused_computation.53 | custom fusion | bytes 8196 | tf_op jit(solution)/shard_map/scatter | solution.py:90
  10.9 13.6 %all_to_all.17 = s32[8,1,256]{2,1,0:T(1,128)S(1)} all-to-all(s32[8,1,256]{2,1,0:T(1,128)S(1)} %bitcast.67), channel_id=1, replica_groups=mesh['dp'=8,'row'=4] {'dp'}, dimensions={0} | all-to-all | bytes 16384 | tf_op jit(solution)/shard_map/all_to_all | solution.py:92
  24.6 8.3 %gather_fusion = bf16[896,1024]{1,0:T(8,128)(2,1)} fusion(bf16[2048,1024]{1,0:T(8,128)(2,1)} %param.17, s32[1024]{0:T(1024)S(1)} %pad_clamp_fusion.1), kind=kCustom, calls=%fused_computation | custom fusion | bytes 3673600 | tf_op jit(solution)/shard_map/jit(_take)/gather | solution.py:93
  32.8 4.5 %all-to-all-start.1 = ((bf16[8,112,1024]{2,1,0:T(8,128)(2,1)}), bf16[8,112,1024]{2,1,0:T(8,128)(2,1)}, u32[]{:S(2)}, u32[]{:S(2)}) async-start(bf16[8,112,1024]{2,1,0:T(8,128)(2,1)} %bitcast.5), calls=%async_computation.1 | async-start | bytes 3670016 | tf_op jit(solution)/shard_map/all_to_all | solution.py:95
  37.6 138.8 %gather_logits.1 = (bf16[8,256,1024]{2,1,0:T(8,128)(2,1)}, bf16[8,256,1024]{2,1,0:T(8,128)(2,1)}, f32[64,2048]{1,0:T(8,128)}) custom-call(bf16[256,1024]{1,0:T(8,128)(2,1)} %q_ref.1, bf16[256,1024]{1,0:T(8,128)(2,1)} %p_ref.1), custom_call_target="tpu_custom_call" | custom-call | tf_op jit(solution)/shard_map/gather_logits/pallas_call | solution.py:328
  178.2 1.3 fusion.27
  179.7 8.8 %gather_fusion.1 = bf16[1152,1024]{1,0:T(8,128)(2,1)S(1)} fusion(bf16[2048,1024]{1,0:T(8,128)(2,1)} %param.17, s32[2048]{0:T(1024)S(1)} %pad_clamp_fusion), kind=kCustom, calls=%fused_computation.1 | custom fusion | bytes 4723200 | tf_op jit(solution)/shard_map/jit(_take)/gather | solution.py:96
  188.5 11.9 %conditional.1 = (bf16[144,1024]{1,0:T(8,128)(2,1)}) conditional(s32[]{:T(128)} %clamp.3, bf16[8,144,1024]{2,1,0:T(8,128)(2,1)S(1)} %bitcast.53, bf16[8,144,1024]{2,1,0:T(8,128)(2,1)S(1)} %bitcast.54, bf16[8,144,1024]{2,1,0:T(8,128)(2,1)S(1)} %bitcast.55, bf16[8,144,1024]{2,1,0:T(8,128)(2,1)S(1)} %bitcast.56, ...), branch_computations={%region_7.8_spmd, %region_8.9_spmd, %region_9.10_spmd, %region_10.... | conditional | bytes 8 | solution.py:98
  188.6 11.6 %spill_4.1 = bf16[144,1024]{1,0:T(8,128)(2,1)} custom-call(bf16[8,144,1024]{2,1,0:T(8,128)(2,1)S(1)} %rows_ref.4), custom_call_target="tpu_custom_call" | custom-call | tf_op jit(solution)/shard_map/cond/branch_4_fun/spill_4/pallas_call | solution.py:65
  200.4 1.8 pad_maximum_fusion
  202.2 5.4 %gather_fusion.2 = bf16[1024,1024]{1,0:T(8,128)(2,1)} fusion(bf16[1040,1024]{1,0:T(8,128)(2,1)S(1)} %pad_maximum_fusion, s32[1024]{0:T(1024)S(1)} %broadcast_clamp_fusion), kind=kCustom, calls=%fused_computation.2 | custom fusion | bytes 4198400 | tf_op jit(solution)/shard_map/jit(_take)/gather | solution.py:104
  207.6 2.2 fusion
  210.4 5.0 %gather_hard.1 = f32[4,8,256]{2,1,0:T(8,128)} custom-call(f32[8,256]{1,0:T(8,128)} %pad.8.x_ref), custom_call_target="tpu_custom_call" | custom-call | tf_op jit(solution)/shard_map/gather_hard/pallas_call | solution.py:510
  215.4 0.8 reduce_sum.90
  218.2 0.7 fusion.19.w_ref
  218.9 1.2 broadcast_in_dim.45.loss_ref
  220.2 35.8 %exchange_weights.1 = (bf16[2,2,64,2176]{3,2,1,0:T(8,128)(2,1)}, bf16[2,2,8,64,256]{4,3,2,1,0:T(8,128)(2,1)}, f32[2,2,8,8,128]{4,3,2,1,0:T(8,128)}) custom-call(bf16[64,2176]{1,0:T(8,128)(2,1)} %fusion.19.w_ref, f32[8,128]{1,0:T(8,128)} %broadcast_in_dim.45.loss_ref), custom_call_target="tpu_custom_call" | custom-call | tf_op jit(solution)/shard_map/exchange_weights/pallas_call | solution.py:460
  256.0 1.5 slice_reduce_fusion.1
  257.5 1.1 slice_convert_fusion.3
  259.7 4.7 %fusion.11 = bf16[256,1024]{1,0:T(8,128)(2,1)} fusion(bf16[4,8,64,256]{3,2,1,0:T(8,128)(2,1)} %bitcast.78, bf16[8,4,64,1024]{3,2,1,0:T(8,128)(2,1)} %bitcast.77), kind=kOutput, calls=%fused_computation.16 | convolution fusion | flops 1074003968 | bytes 5767168 | tf_op jit(solution)/shard_map/dot_general | solution.py:579
  264.4 3.8 %fusion.10 = bf16[256,1024]{1,0:T(8,128)(2,1)} fusion(bf16[2048,1024]{1,0:T(8,128)(2,1)S(1)} %bitcast.76, bf16[256,2176]{1,0:T(8,128)(2,1)S(1)} %bitcast.63, bf16[1024,1024]{1,0:T(8,128)(2,1)} %gather_fusion.2, f32[256]{0:T(256)S(1)} %bitcast.72, f32[256]{0:T(256)S(1)} %bitcast.73, f32[256]{0:T(256)S(1)} %bitcast.74, f32[256]{0:T(256)S(1)} %bitcast.75), kind=kOutput, calls=%fused_computation.15 | convolution fusion | flops 1077149696 | bytes 7868416 | tf_op jit(solution)/shard_map/dot_general | solution.py:572
  (58 shorter events, 6.4 us)
Async XLA Ops:
  0.6 177.5 %copy-start = (s32[16]{0:T(128)S(1)}, s32[16]{0:T(128)}, u32[]{:S(2)}) copy-start(s32[16]{0:T(128)} %param.21) | copy-start | bytes 196
  32.8 4.6 %copy-start.2 = (bf16[256,1024]{1,0:T(8,128)(2,1)S(1)}, bf16[256,1024]{1,0:T(8,128)(2,1)}, u32[]{:S(2)}) copy-start(bf16[256,1024]{1,0:T(8,128)(2,1)} %q_ref.1) | copy-start | bytes 1572868
  32.8 167.6 %all-to-all-start.1 = ((bf16[8,112,1024]{2,1,0:T(8,128)(2,1)}), bf16[8,112,1024]{2,1,0:T(8,128)(2,1)}, u32[]{:S(2)}, u32[]{:S(2)}) async-start(bf16[8,112,1024]{2,1,0:T(8,128)(2,1)} %bitcast.5), calls=%async_computation.1 | async-start | bytes 3670016 | tf_op jit(solution)/shard_map/all_to_all | solution.py:95
  37.3 139.4 %copy-start.5 = (s32[256]{0:T(256)S(1)}, s32[256]{0:T(256)}, u32[]{:S(2)}) copy-start(s32[256]{0:T(256)} %param.20) | copy-start | bytes 3076
  207.6 8.9 %copy-start.1 = (f32[64,2048]{1,0:T(8,128)S(1)}, f32[64,2048]{1,0:T(8,128)}, u32[]{:S(2)}) copy-start(f32[64,2048]{1,0:T(8,128)} %get-tuple-element.27) | copy-start | bytes 1572868
  259.7 4.8 %copy-start.3 = (bf16[2,2,64,2176]{3,2,1,0:T(8,128)(2,1)S(1)}, bf16[2,2,64,2176]{3,2,1,0:T(8,128)(2,1)}, u32[]{:S(2)}) copy-start(bf16[2,2,64,2176]{3,2,1,0:T(8,128)(2,1)} %get-tuple-element.30) | copy-start | bytes 3342340
  259.7 4.8 %copy-start.4 = (bf16[8,256,1024]{2,1,0:T(8,128)(2,1)S(1)}, bf16[8,256,1024]{2,1,0:T(8,128)(2,1)}, u32[]{:S(2)}) copy-start(bf16[8,256,1024]{2,1,0:T(8,128)(2,1)} %get-tuple-element.31) | copy-start | bytes 12582916
where the time goes:
time: 270 us; the launch traced here: 269 us
  Pallas kernels  191 us (71%)
  local copies, waits for them, and re-layouts  32.5 us (12%)
  other arithmetic  15.4 us (6%)
  blocking collectives  13.6 us (5%)
  matrix products  8.51 us (3%)
  starting transfers between devices  4.45 us (2%)
  between operations  3.38 us (1%)
    pallas_call x1, Pallas kernels, gather_and_logits(): pl.pallas_call(functools.partial(gather_kernel, n, n_row), name='gather_l...  139 us
    pallas_call x1, Pallas kernels, exchange_weights(): pl.pallas_call(functools.partial(weights_kernel, n, n_row, columns), name...  35.8 us
    all_to_all x1, blocking collectives, fetch_hard(): lax.all_to_all(requests, 'dp', split_axis=0, concat_axis=0, tiled=True)  13.6 us
    pallas_call x1, Pallas kernels, spill(): pl.pallas_call(functools.partial(spill_kernel, n, hot), name=f'spill_{hot...  11.6 us
    gather x1, local copies, waits for them, and re-layouts, fetch_hard(): jnp.take(cached, asked_rows[:, common:].reshape(-1), axis=0, mode='clip')  8.85 us
    gather x1, local copies, waits for them, and re-layouts, fetch_hard(): jnp.take(cached, asked_rows[:, :common].reshape(-1), axis=0, mode='clip')  8.26 us
  transfers between devices with their start and end apart: 1, of which 0 were waited for; matrix products, arithmetic and copies ran while one was open for 4% of the time, Pallas kernels for 56%

commit v1 on v0

--- a/solution.py
+++ b/solution.py
@@ -585,6 +585,558 @@
     return (mean_loss, query_grad.astype(jnp.bfloat16), passage_grad.astype(jnp.bfloat16))
 
 
+def fused_kernel(n, n_row, scale, sources_ref, note_ref, q_ref, p_ref, cache_ref,
+                 qgrad, pgrad, loss_out,
+                 qall, cache, picked, chosen, notes, lpart, cpart, ypart, peak, mass,
+                 stat_own, stat_all, wts, acc, pacc, xsend, xrecv, zsend, zrecv,
+                 loss_own, loss_all, loss_mine, loss_beside,
+                 gsend, grecv, nsend, nrecv, csend, crecv, ysend, yrecv, ssend, srecv,
+                 wsend, wrecv, xs, xr, zs, zr, lsend, lrecv, own_sem):
+    me = lax.axis_index("dp")
+    r = lax.axis_index("row")
+    lines = n // 2
+    a = me // 2
+    b = me % 2
+    n_line = n_row // 2
+    y = r // 2
+    core = r % 2
+    across = a * 2 + 1 - b
+    partner = y * 2 + 1 - core
+    rows, width = q_ref.shape
+    columns = p_ref.shape[0]
+    half = rows // 2
+    slots = cache.shape[0]
+    tile = min(width, 256)
+    f32 = jnp.float32
+    bf16 = jnp.bfloat16
+
+    load_cache = pltpu.make_async_copy(cache_ref, cache, own_sem.at[0])
+    load_cache.start()
+    own_q = pltpu.make_async_copy(q_ref, qall.at[me], own_sem.at[1])
+    own_q.start()
+
+    barrier = pltpu.get_barrier_semaphore()
+    for j in range(1, n):
+        pl.semaphore_signal(
+            barrier, inc=1, device_id=(lax.rem(me + j, n), r), device_id_type=MESH
+        )
+    for k in range(1, n_line):
+        pl.semaphore_signal(
+            barrier, inc=1, device_id=(me, lax.rem(r + 2 * k, n_row)), device_id_type=MESH
+        )
+    pl.semaphore_signal(barrier, inc=1, device_id=(me, partner), device_id_type=MESH)
+    pl.semaphore_wait(barrier, n + n_line - 1)
+
+    def remote(src, dst, send, recv, to):
+        return pltpu.make_async_remote_copy(
+            src_ref=src, dst_ref=dst, send_sem=send, recv_sem=recv,
+            device_id=to, device_id_type=MESH,
+        )
+
+    def query_copy(kind, blk, first=False):
+        to = (across, me + 2, me - 2)[kind]
+        return remote(
+            q_ref if first else qall.at[blk], qall.at[blk],
+            gsend.at[kind, blk], grecv.at[blk], (to, r),
+        )
+
+    def note_copy(j):
+        to = lax.rem(me + j, n)
+        return remote(
+            note_ref.at[to], notes.at[me], nsend.at[j - 1], nrecv.at[j - 1], (to, r)
+        )
+
+    def core_copy(blk):
+        return remote(
+            lpart.at[blk, 1 - core], cpart.at[blk], csend.at[blk], crecv.at[blk], (me, partner)
+        )
+
+    def line_copy(blk, k):
+        return remote(
+            ypart.at[blk, y], ypart.at[blk, y], ysend.at[blk, k - 1], yrecv.at[blk, k - 1],
+            (me, lax.rem(r + 2 * k, n_row)),
+        )
+
+    def stat_copy(j):
+        to = lax.rem(me + j, n)
+        return remote(stat_own, stat_all.at[me], ssend.at[j - 1], srecv.at[j - 1], (to, r))
+
+    def weight_copy(blk):
+        return remote(
+            wts.at[blk, core], wts.at[blk, core], wsend.at[blk], wrecv.at[blk], (me, partner)
+        )
+
+    def cross_copy(zi):
+        return remote(xsend.at[zi], xrecv.at[zi], xs.at[zi], xr.at[zi], (across, r))
+
+    def up_copy(zi):
+        return remote(zsend.at[zi], zrecv.at[zi], zs.at[zi], zr.at[zi], (me + 2, r))
+
+    def down_copy(zi, last):
+        slot = zi + last * (lines - zi)
+        return remote(zsend.at[zi], zrecv.at[slot], zs.at[zi], zr.at[slot], (me - 2, r))
+
+    def loss_copy(j):
+        to = lax.rem(me + j, n)
+        return remote(loss_own, loss_all.at[me], lsend.at[j - 1], lrecv.at[j - 1], (to, r))
+
+    loss_core = remote(loss_mine, loss_beside, lsend.at[n - 1], lrecv.at[n - 1], (me, partner))
+
+    def group(s, body):
+        @pl.loop(0, 2)
+        def _(k):
+            zi = a + (2 * k - 1) * s
+
+            @pl.when((zi >= 0) & (zi < lines) & (k + s > 0))
+            def _():
+                body(zi)
+
+    lane = lax.broadcasted_iota(jnp.int32, (1, half), 1)
+    sub = lax.broadcasted_iota(jnp.int32, (BLOCK, half), 0)
+    at_lanes = pl.ds(pl.multiple_of(core * half, half), half)
+
+    def pick(blk):
+        wide = lax.broadcasted_iota(jnp.int32, (rows, rows), 0)
+        high = lax.broadcasted_iota(jnp.int32, (rows, rows), 1)
+        named = jnp.sum(
+            jnp.where(wide == high, notes[blk, 0:1, :], 0.0), axis=1, keepdims=True
+        )
+        number = lax.broadcasted_iota(jnp.int32, (rows, slots), 1).astype(f32)
+        chosen[...] = jnp.where(number == named, 1.0, 0.0).astype(bf16)
+        for t in range(0, width, tile):
+            picked[blk, :, t:t + tile] = jnp.dot(
+                chosen[...], cache[:, t:t + tile], preferred_element_type=f32
+            ).astype(bf16)
+
+    over_width = (((1,), (1,)), ((), ()))
+    over_rows = (((0,), (0,)), ((), ()))
+
+    def multiply(blk):
+        q = qall[blk]
+        logits = lax.dot_general(p_ref[...], q, over_width, preferred_element_type=f32)
+        for h in range(2):
+            cut = slice(h * half, (h + 1) * half)
+            mixed = lax.dot_general(
+                picked[blk, cut, :], q[cut, :], over_width, preferred_element_type=f32
+            )
+            down = lax.broadcasted_iota(jnp.int32, (half, half), 0)
+            right = lax.broadcasted_iota(jnp.int32, (half, half), 1)
+            hard = jnp.sum(jnp.where(down == right, mixed, 0.0), axis=0, keepdims=True)
+            lpart[blk, h, 0:columns, :] = logits[:, cut]
+            lpart[blk, h, columns:columns + 8, :] = jnp.broadcast_to(hard, (8, half))
+        core_copy(blk).start()
+
+    def add_core(blk):
+        core_copy(blk).wait_recv()
+        ypart[blk, y] = lpart[blk, core] + cpart[blk]
+        for k in range(1, n_line):
+            line_copy(blk, k).start()
+
+    def scored(blk, t):
+        cut = slice(t * BLOCK, (t + 1) * BLOCK)
+        values = scale * lpart[blk, core, cut, :]
+        source = sources_ref[me * (columns // BLOCK) + t].astype(f32)
+        positive = (sub + (me * columns + t * BLOCK)) == (lane + (blk * rows + core * half))
+        allowed = (notes[blk, 1:2, at_lanes] != source) | positive
+        return jnp.where(allowed, values, NEG_FILL), positive
+
+    def scored_hard(blk):
+        values = scale * lpart[blk, core, columns:columns + 1, :]
+        return jnp.where(notes[blk, 0:1, at_lanes] >= 0.0, values, NEG_FILL)
+
+    parts = columns // BLOCK
+
+    def local_stats(blk):
+        for k in range(1, n_line):
+            line_copy(blk, k).wait_recv()
+        total = ypart[blk, 0]
+        for k in range(1, n_line):
+            total = total + ypart[blk, k]
+        lpart[blk, core] = total
+        hard = scored_hard(blk)
+        blocks = [scored(blk, t)[0] for t in range(parts)]
+        top = hard
+        for block in blocks:
+            top = jnp.maximum(top, jnp.max(block, axis=0, keepdims=True))
+        added = jnp.exp(hard - top)
+        for block in blocks:
+            added = added + jnp.sum(jnp.exp(block - top), axis=0, keepdims=True)
+        stat_own[0, pl.ds(blk, 1), :] = top
+        stat_own[1, pl.ds(blk, 1), :] = added
+
+    @pl.when(a < lines - 1)
+    def _():
+        query_copy(1, me, True).start()
+
+    @pl.when(a > 0)
+    def _():
+        query_copy(2, me, True).start()
+
+    query_copy(0, me, True).start()
+    for j in range(1, n):
+        note_copy(j).start()
+    notes[me] = note_ref[me]
+    load_cache.wait()
+    own_q.wait()
+    for j in range(1, n):
+        note_copy(j).wait_recv()
+
+    def mine(f):
+        return lambda zi: f(zi * 2 + b)
+
+    def theirs(f):
+        return lambda zi: f(zi * 2 + 1 - b)
+
+    def relay(zi):
+        blk = zi * 2 + b
+        query_copy(0, blk).wait_recv()
+
+        @pl.when((zi < a) & (a < lines - 1))
+        def _():
+            query_copy(1, blk).start()
+
+        @pl.when((zi > a) & (a > 0))
+        def _():
+            query_copy(2, blk).start()
+
+        query_copy(0, blk).start()
+
+    def from_across(blk):
+        query_copy(0, blk).wait_recv()
+        multiply(blk)
+
+    pick(me)
+    multiply(me)
+    group(1, mine(pick))
+    pick(across)
+
+    @pl.loop(1, lines)
+    def _(s):
+        group(s, relay)
+        group(s, mine(multiply))
+        group(s - 1, theirs(from_across))
+        group(s - 1, mine(add_core))
+        group(s - 1, theirs(add_core))
+
+        @pl.when(s < lines - 1)
+        def _():
+            group(s + 1, mine(pick))
+
+        group(s, theirs(pick))
+
+        @pl.when(s > 1)
+        def _():
+            group(s - 2, mine(local_stats))
+            group(s - 2, theirs(local_stats))
+
+    if lines > 1:
+        group(lines - 2, mine(local_stats))
+        group(lines - 2, theirs(local_stats))
+    group(lines - 1, mine(add_core))
+    group(lines - 1, theirs(from_across))
+    group(lines - 1, theirs(add_core))
+    group(lines - 1, mine(local_stats))
+    group(lines - 1, theirs(local_stats))
+
+    for j in range(1, n):
+        stat_copy(j).start()
+    stat_all[me] = stat_own[...]
+    for j in range(1, n):
+        stat_copy(j).wait_recv()
+    top = stat_all[0, 0]
+    for j in range(1, n):
+        top = jnp.maximum(top, stat_all[j, 0])
+    total = stat_all[0, 1] * jnp.exp(stat_all[0, 0] - top)
+    for j in range(1, n):
+        total = total + stat_all[j, 1] * jnp.exp(stat_all[j, 0] - top)
+    peak[...] = top
+    mass[...] = total
+
+    def weigh(blk):
+        high = peak[pl.ds(blk, 1), :]
+        whole = mass[pl.ds(blk, 1), :]
+        for t in range(parts):
+            masked, positive = scored(blk, t)
+            weight = jnp.exp(masked - high) / whole - positive.astype(f32)
+            wts[blk, core, t * BLOCK:(t + 1) * BLOCK, :] = weight.astype(bf16)
+        hard = jnp.exp(scored_hard(blk) - high) / whole
+        wts[blk, core, columns:columns + 16, :] = jnp.broadcast_to(hard, (16, half)).astype(bf16)
+        weight_copy(blk).start()
+
+    @pl.loop(0, lines)
+    def _(k):
+        group(lines - 1 - k, theirs(weigh))
+        group(lines - 1 - k, mine(weigh))
+
+    def gradient(blk, store):
+        down = lax.broadcasted_iota(jnp.int32, (half, half), 0)
+        right = lax.broadcasted_iota(jnp.int32, (half, half), 1)
+        for h in range(2):
+            hard = wts[blk, h, columns:columns + 1, :].astype(f32)
+            diagonal = jnp.where(down == right, hard, 0.0).astype(bf16)
+            cut = slice(h * half, (h + 1) * half)
+            out = lax.dot_general(
+                wts[blk, h, 0:columns, :], p_ref[...], over_rows, preferred_element_type=f32
+            )
+            out = out + jnp.dot(diagonal, picked[blk, cut, :], preferred_element_type=f32)
+            store(cut, out)
+
+    def send_across(zi):
+        blk = zi * 2 + 1 - b
+        weight_copy(blk).wait_recv()
+
+        def store(cut, out):
+            xsend[zi, cut, :] = out.astype(bf16)
+
+        gradient(blk, store)
+        cross_copy(zi).start()
+
+    @pl.loop(0, lines)
+    def _(k):
+        group(lines - 1 - k, send_across)
+
+    positive_logit = jnp.zeros((1, half), f32)
+    for t in range(parts):
+        masked, positive = scored(me, t)
+        positive_logit = positive_logit + jnp.sum(
+            jnp.where(positive, masked, 0.0), axis=0, keepdims=True
+        )
+    losses = peak[pl.ds(me, 1), :] + jnp.log(mass[pl.ds(me, 1), :]) - positive_logit
+    loss_own[...] = jnp.broadcast_to(losses, (8, half))
+    for j in range(1, n):
+        loss_copy(j).start()
+    loss_all[me] = loss_own[...]
+
+    pacc[...] = jnp.zeros_like(pacc)
+
+    def passage_terms(blk):
+        both = jnp.concatenate([wts[blk, 0, 0:columns, :], wts[blk, 1, 0:columns, :]], axis=1)
+        for t in range(0, width, tile):
+            pacc[:, t:t + tile] += jnp.dot(
+                both, qall[blk, :, t:t + tile], preferred_element_type=f32
+            )
+
+    def store_acc(cut, out):
+        acc[cut, :] = out
+
+    def pass_on(s):
+        def body(zi):
+            blk = zi * 2 + b
+            weight_copy(blk).wait_recv()
+            gradient(blk, store_acc)
+            passage_terms(blk)
+            passage_terms(zi * 2 + 1 - b)
+            cross_copy(zi).wait_recv()
+            acc[...] += xrecv[zi].astype(f32)
+
+            @pl.when((zi > a) & (a > 0))
+            def _():
+                up_copy(zi).wait_recv()
+                acc[...] += zrecv[zi].astype(f32)
+
+            @pl.when((zi < a) & (a < lines - 1))
+            def _():
+                down_copy(zi, 0).wait_recv()
+                acc[...] += zrecv[zi].astype(f32)
+
+            zsend[zi] = acc[...].astype(bf16)
+
+            @pl.when(zi > a)
+            def _():
+                up_copy(zi).start()
+
+            @pl.when((zi < a) & (s == 1))
+            def _():
+                down_copy(zi, 1).start()
+
+            @pl.when((zi < a) & (s > 1))
+            def _():
+                down_copy(zi, 0).start()
+
+        return body
+
+    @pl.loop(0, lines - 1)
+    def _(k):
+        s = lines - 1 - k
+        group(s, pass_on(s))
+
+    weight_copy(me).wait_recv()
+    gradient(me, store_acc)
+    passage_terms(me)
+    passage_terms(across)
+    pgrad[...] = pacc[...].astype(bf16)
+
+    for j in range(1, n):
+        loss_copy(j).wait_recv()
+    sums = loss_all[0]
+    for j in range(1, n):
+        sums = sums + loss_all[j]
+    loss_mine[...] = sums
+    loss_core.start()
+    loss_core.wait_recv()
+    loss_out[...] = jnp.broadcast_to(
+        jnp.sum(loss_mine[...] + loss_beside[...], axis=1, keepdims=True), (8, half)
+    )
+
+    cross_copy(a).wait_recv()
+    acc[...] += xrecv[a].astype(f32)
+
+    @pl.when(a > 0)
+    def _():
+        up_copy(a).wait_recv()
+        acc[...] += zrecv[a].astype(f32)
+
+    @pl.when(a < lines - 1)
+    def _():
+        down_copy(a, 1).wait_recv()
+        acc[...] += zrecv[lines].astype(f32)
+
+    qgrad[...] = acc[...].astype(bf16)
+
+    query_copy(0, me, True).wait_send()
+
+    @pl.when(a < lines - 1)
+    def _():
+        query_copy(1, me, True).wait_send()
+
+    @pl.when(a > 0)
+    def _():
+        query_copy(2, me, True).wait_send()
+
+    def sent(zi):
+        blk = zi * 2 + b
+
+        @pl.when((zi < a) & (a < lines - 1))
+        def _():
+            query_copy(1, blk).wait_send()
+
+        @pl.when((zi > a) & (a > 0))
+        def _():
+            query_copy(2, blk).wait_send()
+
+        query_copy(0, blk).wait_send()
+
+        @pl.when(zi > a)
+        def _():
+            up_copy(zi).wait_send()
+
+        @pl.when(zi < a)
+        def _():
+            down_copy(zi, 0).wait_send()
+
+    @pl.loop(1, lines)
+    def _(s):
+        group(s, sent)
+
+    @pl.loop(0, lines)
+    def _(zi):
+        cross_copy(zi).wait_send()
+
+    @pl.loop(0, n)
+    def _(blk):
+        core_copy(blk).wait_send()
+        weight_copy(blk).wait_send()
+        for k in range(1, n_line):
+            line_copy(blk, k).wait_send()
+
+    for j in range(1, n):
+        note_copy(j).wait_send()
+        stat_copy(j).wait_send()
+        loss_copy(j).wait_send()
+    loss_core.wait_send()
+
+
+def fused(queries, passages, cached, notes, block_source, n, n_row, scale):
+    rows, width = queries.shape
+    columns = passages.shape[0]
+    slots = cached.shape[0]
+    lines = n // 2
+    n_line = n_row // 2
+    half = rows // 2
+    f32 = jnp.float32
+    bf16 = jnp.bfloat16
+    vmem = pl.BlockSpec(memory_space=pltpu.VMEM)
+    mem = pltpu.VMEM
+    dma = pltpu.SemaphoreType.DMA
+    return pl.pallas_call(
+        functools.partial(fused_kernel, n, n_row, scale),
+        name="fused_loss",
+        out_shape=(
+            jax.ShapeDtypeStruct((rows, width), bf16),
+            jax.ShapeDtypeStruct((columns, width), bf16),
+            jax.ShapeDtypeStruct((8, half), f32),
+        ),
+        in_specs=[
+            pl.BlockSpec(memory_space=pltpu.SMEM), vmem, vmem, vmem,
+            pl.BlockSpec(memory_space=pl.ANY),
+        ],
+        out_specs=(vmem, vmem, vmem),
+        scratch_shapes=[
+            mem((n, rows, width), bf16),
+            mem((slots, width), bf16),
+            mem((n, rows, width), bf16),
+            mem((rows, slots), bf16),
+            mem((n, 2, rows), f32),
+            mem((n, 2, columns + 8, half), f32),
+            mem((n, columns + 8, half), f32),
+            mem((n, n_line, columns + 8, half), f32),
+            mem((n, half), f32),
+            mem((n, half), f32),
+            mem((2, n, half), f32),
+            mem((n, 2, n, half), f32),
+            mem((n, 2, columns + 16, half), bf16),
+            mem((rows, width), f32),
+            mem((columns, width), f32),
+            mem((lines, rows, width), bf16),
+            mem((lines, rows, width), bf16),
+            mem((lines, rows, width), bf16),
+            mem((lines + 1, rows, width), bf16),
+            mem((8, half), f32),
+            mem((n, 8, half), f32),
+            mem((8, half), f32),
+            mem((8, half), f32),
+            dma((3, n)), dma((n,)),
+            dma((n - 1,)), dma((n - 1,)),
+            dma((n,)), dma((n,)),
+            dma((n, max(n_line - 1, 1))), dma((n, max(n_line - 1, 1))),
+            dma((n - 1,)), dma((n - 1,)),
+            dma((n,)), dma((n,)),
+            dma((lines,)), dma((lines,)),
+            dma((lines,)), dma((lines + 1,)),
+            dma((n,)), dma((n,)),
+            dma((2,)),
+        ],
+        compiler_params=pltpu.CompilerParams(
+            collective_id=0, has_side_effects=True, vmem_limit_bytes=60 * 2**20
+        ),
+    )(block_source, notes, queries, passages, cached)
+
+
+def on_device_fused(queries, passages, cached, hard_shard, hard_row, query_source, block_source):
+    n = lax.axis_size("dp")
+    n_row = lax.axis_size("row")
+    rows = queries.shape[0]
+    shard = hard_shard.T[None]
+    named = jnp.where(
+        shard == jnp.arange(n, dtype=jnp.int32)[:, None, None], hard_row.T[None] + 1, 0
+    )
+    named = jnp.sum(named, axis=1) - 1
+    notes = jnp.stack(
+        [named, jnp.broadcast_to(query_source[None], (n, rows))], axis=1
+    ).astype(jnp.float32)
+    query_grad, passage_grad, losses = fused(
+        queries, passages, cached, notes, block_source, n, n_row, 1.0 / math.sqrt(D)
+    )
+    return (losses[0, 0] / (rows * n), query_grad, passage_grad)
+
+
+def fits(n, n_row, rows, width, slots):
+    blocks = 2 * (n * rows * width * 2 + (2 * n + 2) * rows * width + slots * width)
+    half = rows // 2
+    scores = n * (3 + n_row // 2) * (rows + 8) * half * 4
+    return blocks + scores < 48 * 2**20
+
+
 def solution(mesh):
     in_specs = (
         P("dp", "row"),
@@ -596,6 +1148,14 @@
         P(),
     )
     out_specs = (P(), P("dp", "row"), P("dp", "row"))
+
+    def body(queries, passages, cached, *rest):
+        rows, width = queries.shape
+        n, n_row = mesh.shape["dp"], mesh.shape["row"]
+        if fits(n, n_row, rows, width, cached.shape[0]):
+            return on_device_fused(queries, passages, cached, *rest)
+        return on_device(queries, passages, cached, *rest)
+
     return jax.shard_map(
-        on_device, mesh=mesh, in_specs=in_specs, out_specs=out_specs, check_vma=False
-    )
+        body, mesh=mesh, in_specs=in_specs, out_specs=out_specs, check_vma=False
+    )

time: 270 us -> 139 us (0.51)
  Pallas kernels: 191 us -> 128 us
  local copies, waits for them, and re-layouts: 32.5 us -> 5.62 us
  blocking collectives: 13.6 us -> 0 us
  other arithmetic: 15.4 us -> 2.01 us
  matrix products: 8.51 us -> 0 us
  starting transfers between devices: 4.45 us -> 0 us
    pallas_call x4 -> x1, Pallas kernels: 191 us -> 128 us  [fused(): pl.pallas_call(functools.partial(fused_kernel, n, n_row, scale), name='fu...]
    gather x3 -> x0, local copies, waits for them, and re-layouts: 22.5 us -> none  [the longest x1 8.85 us: fetch_hard(): jnp.take(cached, asked_rows[:, common:].reshape(-1), axis=0, mode='clip')]
    all_to_all x1 -> x0, blocking collectives: 13.6 us -> none  [fetch_hard(): lax.all_to_all(requests, 'dp', split_axis=0, concat_axis=0, tiled=True)]
    dot_general x2 -> x0, matrix products: 8.51 us -> none  [the longest x1 4.74 us: on_device(): lax.dot_general(wcol.reshape(n_row, n_data, part, columns), qall.reshape(...]
    reduce_sum x7 -> x1, other arithmetic: 5.83 us -> 0.7 us  [on_device_fused(): named = jnp.sum(named, axis=1) - 1]
    all_to_all x1 -> x0, starting transfers between devices: 4.45 us -> none  [fetch_hard(): lax.all_to_all(picked, 'dp', split_axis=0, concat_axis=0, tiled=True)]
    scatter x1 -> x0, local copies, waits for them, and re-layouts: 4.32 us -> none  [fetch_hard(): jnp.zeros((n_data * capacity,), jnp.int32).at[target].set(wanted)]
    another operation x3 -> x0, other arithmetic: 3.08 us -> none
  transfers between devices with their start and end apart: 1 -> 0, of which waited for: 0 -> 0; matrix products, arithmetic and copies ran while one was open for 4% -> 0% of each run, Pallas kernels for 56% -> 0%
where the time goes in v1:
time: 139 us; the launch traced here: 138 us
  Pallas kernels  128 us (92%)
  local copies, waits for them, and re-layouts  5.62 us (4%)
  between operations  2.43 us (2%)
  other arithmetic  2.01 us (1%)
    pallas_call x1, Pallas kernels, fused(): pl.pallas_call(functools.partial(fused_kernel, n, n_row, scale), name='fu...  128 us
    unnamed x2, local copies, waits for them, and re-layouts  3.74 us

profile of v1, /device:TPU:0, one launch (start us, length us, event | category | flops | bytes accessed | tf_op | source)
XLA Modules:
  0.0 138.4 jit_solution(7463495897006607204)
XLA Ops:
  0.6 0.7 add_bitcast_fusion
  1.3 0.7 select_reduce_fusion
  2.0 0.7 stack_broadcast_in_dim.2
  2.7 0.6 add_convert_fusion.note_ref
  3.3 128.4 %fused_loss.1 = (bf16[256,1024]{1,0:T(8,128)(2,1)}, bf16[256,1024]{1,0:T(8,128)(2,1)}, f32[8,128]{1,0:T(8,128)}) custom-call(s32[16]{0:T(128)} %sources_ref.1, f32[8,2,256]{2,1,0:T(2,128)} %add_convert_fusion.note_ref, bf16[256,1024]{1,0:T(8,128)(2,1)} %q_ref.1, bf16[256,1024]{1,0:T(8,128)(2,1)} %p_ref.1, bf16[2048,1024]{1,0:T(8,128)(2,1)} %cache_ref.1), custom_call_target="tpu_custom_call" | custom-call | tf_op jit(solution)/shard_map/fused_loss/pallas_call | solution.py:1061
  131.7 1.2 slice.3
  133.6 1.9 %copy.12 = bf16[256,1024]{1,0:T(8,128)(2,1)} copy(bf16[256,1024]{1,0:T(8,128)(2,1)} %get-tuple-element.13) | data formatting | bytes 1048576
  135.4 1.9 %copy.13 = bf16[256,1024]{1,0:T(8,128)(2,1)} copy(bf16[256,1024]{1,0:T(8,128)(2,1)} %get-tuple-element.14) | data formatting | bytes 1048576
  (2 shorter events, 0.0 us)

commit v2 on v0

--- a/solution.py
+++ b/solution.py
@@ -585,6 +585,729 @@
     return (mean_loss, query_grad.astype(jnp.bfloat16), passage_grad.astype(jnp.bfloat16))
 
 
+def fused_kernel(n, n_row, stages, direct, scale, sources_ref, shard_ref, row_ref, source_ref,
+                 q_ref, p_ref, cache_ref, qgrad, pgrad, loss_out,
+                 qall, cache, picked, chosen, note_own, notes, unit_notes, lpart, cpart, ypart,
+                 peak, mass, stat_own, stat_all, wts, acc, pacc, xsend, xrecv, zsend, zrecv,
+                 lsum, lrest, loss_own, loss_all, loss_mine, loss_beside,
+                 gsend, grecv, nsend, nrecv, csend, crecv, ysend, yrecv, ssend, srecv,
+                 wsend, wrecv, xs, xr, zs, zr, ms, mr, lsend, lrecv, own_sem):
+    me = lax.axis_index("dp")
+    r = lax.axis_index("row")
+    lines = n // 2
+    far = lines - 1
+    period = max(far, 1)
+    a = me // 2
+    b = me % 2
+    n_line = n_row // 2
+    y = r // 2
+    core = r % 2
+    across = a * 2 + 1 - b
+    partner = y * 2 + 1 - core
+    rows, width = q_ref.shape
+    columns = p_ref.shape[0]
+    parts = columns // BLOCK
+    part = rows // stages
+    pair = 2 * part
+    rest = part - direct
+    slots = cache.shape[0]
+    tile = min(width, 256)
+    f32 = jnp.float32
+    bf16 = jnp.bfloat16
+
+    load_cache = pltpu.make_async_copy(cache_ref, cache, own_sem.at[0])
+    load_cache.start()
+
+    barrier = pltpu.get_barrier_semaphore()
+    for j in range(1, n):
+        pl.semaphore_signal(
+            barrier, inc=1, device_id=(lax.rem(me + j, n), r), device_id_type=MESH
+        )
+    for k in range(1, n_line):
+        pl.semaphore_signal(
+            barrier, inc=1, device_id=(me, lax.rem(r + 2 * k, n_row)), device_id_type=MESH
+        )
+    pl.semaphore_signal(barrier, inc=1, device_id=(me, partner), device_id_type=MESH)
+
+    own_q = [
+        pltpu.make_async_copy(
+            q_ref.at[pl.ds(q * part, part)], qall.at[a, q, b], own_sem.at[1 + q]
+        )
+        for q in range(stages)
+    ]
+    for copy in own_q:
+        copy.start()
+    source = source_ref[...].astype(f32)
+    for s in range(n):
+        named = jnp.where(shard_ref[...] == s, row_ref[...] + 1, 0)
+        note_own[s, 0:1, :] = jnp.sum(named.astype(f32), axis=0, keepdims=True) - 1.0
+        note_own[s, 1:2, :] = source
+    pacc[...] = jnp.zeros_like(pacc)
+    lsum[...] = jnp.zeros_like(lsum)
+    stat_own[...] = jnp.zeros_like(stat_own)
+    pl.semaphore_wait(barrier, n + n_line - 1)
+
+    def remote(src, dst, send, recv, to):
+        return pltpu.make_async_remote_copy(
+            src_ref=src, dst_ref=dst, send_sem=send, recv_sem=recv,
+            device_id=to, device_id_type=MESH,
+        )
+
+    head = pl.ds(0, direct)
+    tail = pl.ds(direct, rest)
+
+    def own_rows(q, start, size):
+        return q_ref.at[pl.ds(pl.multiple_of(q * part + start, 16), size)]
+
+    def column_copy(up, zi, q, first=False):
+        at = qall.at[zi, q, b]
+        return remote(
+            own_rows(q, 0, part) if first else at, at, gsend.at[1 if up else 2, zi, q],
+            grecv.at[0, zi, q], (me + 2 if up else me - 2, r),
+        )
+
+    def head_copy(zi, q, first=False):
+        at = qall.at[zi, q, b, head]
+        return remote(
+            own_rows(q, 0, direct) if first else at, at, gsend.at[0, zi, q],
+            grecv.at[1, zi, q], (across, r),
+        )
+
+    def tail_copy(q):
+        return remote(
+            own_rows(q, direct, rest), qall.at[a, q, b, tail], gsend.at[3, a, q],
+            grecv.at[2, a, q], (across, r),
+        )
+
+    def tail_relay(up, zi, q):
+        at = qall.at[zi, q, 1 - b, tail]
+        return remote(
+            at, at, gsend.at[4 if up else 5, zi, q], grecv.at[2, zi, q],
+            (me + 2 if up else me - 2, r),
+        )
+
+    def note_copy(j):
+        to = lax.rem(me + j, n)
+        return remote(
+            note_own.at[to], notes.at[me], nsend.at[j - 1], nrecv.at[j - 1], (to, r)
+        )
+
+    def core_copy(zi, q):
+        return remote(
+            lpart.at[q, zi], cpart.at[q, zi // 2], csend.at[q, zi], crecv.at[q, zi],
+            (me, partner),
+        )
+
+    def line_copy(zi, q, k):
+        at = ypart.at[q, zi // 2, y]
+        return remote(
+            at, at, ysend.at[q, zi, k - 1], yrecv.at[q, zi, k - 1],
+            (me, lax.rem(r + 2 * k, n_row)),
+        )
+
+    def stat_copy(j, q):
+        to = lax.rem(me + j, n)
+        return remote(
+            stat_own.at[q], stat_all.at[q, me], ssend.at[q, j - 1], srecv.at[q, j - 1], (to, r)
+        )
+
+    def weight_copy(zi, q):
+        at = wts.at[q, zi]
+        return remote(at, at, wsend.at[q, zi], wrecv.at[q, zi], (me, partner))
+
+    def cross_copy(zi, q):
+        return remote(xsend.at[q, zi], xrecv.at[q, zi], xs.at[q, zi], xr.at[q, zi], (across, r))
+
+    def up_copy(zi, q):
+        return remote(zsend.at[q, zi], zrecv.at[q, zi], zs.at[q, zi], zr.at[q, zi], (me + 2, r))
+
+    def down_copy(zi, q, last):
+        slot = zi + last * (lines - zi)
+        return remote(
+            zsend.at[q, zi], zrecv.at[q, slot], zs.at[q, zi], zr.at[q, slot], (me - 2, r)
+        )
+
+    def rest_copy(q):
+        return remote(zsend.at[q, a, pl.ds(part, rest)], lrest.at[q], ms.at[q], mr.at[q], (across, r))
+
+    def loss_copy(j):
+        to = lax.rem(me + j, n)
+        return remote(loss_own, loss_all.at[me], lsend.at[j - 1], lrecv.at[j - 1], (to, r))
+
+    loss_core = remote(loss_mine, loss_beside, lsend.at[n - 1], lrecv.at[n - 1], (me, partner))
+
+    def group(s, body):
+        if s == 0:
+            body(a)
+            return
+
+        @pl.loop(0, 2)
+        def _(k):
+            zi = a + (2 * k - 1) * s
+
+            @pl.when((zi >= 0) & (zi < lines))
+            def _():
+                body(zi)
+
+    def owned(body):
+        def f(zi):
+            @pl.when(zi % 2 == core)
+            def _():
+                body(zi)
+
+        return f
+
+    lane = lax.broadcasted_iota(jnp.int32, (1, pair), 1)
+    right_half = (lane >= part).astype(jnp.int32)
+    sub = lax.broadcasted_iota(jnp.int32, (BLOCK, pair), 0)
+    over_width = (((1,), (1,)), ((), ()))
+    over_rows = (((0,), (0,)), ((), ()))
+
+    def diagonal():
+        down = lax.broadcasted_iota(jnp.int32, (pair, pair), 0)
+        right = lax.broadcasted_iota(jnp.int32, (pair, pair), 1)
+        return down == right
+
+    def start_own(q):
+        @pl.when(a < far)
+        def _():
+            column_copy(True, a, q, True).start()
+
+        @pl.when(a > 0)
+        def _():
+            column_copy(False, a, q, True).start()
+
+        tail_copy(q).start()
+        head_copy(a, q, True).start()
+
+    def turn(q):
+        tail_copy(q).wait_recv()
+
+        @pl.when(a < far)
+        def _():
+            tail_relay(True, a, q).start()
+
+        @pl.when(a > 0)
+        def _():
+            tail_relay(False, a, q).start()
+
+    def relay(s):
+        def column(q):
+            def body(zi):
+                column_copy(True, zi, q).wait_recv()
+
+                @pl.when((zi < a) & (a < far))
+                def _():
+                    column_copy(True, zi, q).start()
+
+                @pl.when((zi > a) & (a > 0))
+                def _():
+                    column_copy(False, zi, q).start()
+
+                head_copy(zi, q).start()
+
+            return body
+
+        def tails(q):
+            def body(zi):
+                tail_relay(True, zi, q).wait_recv()
+
+                @pl.when((zi < a) & (a < far))
+                def _():
+                    tail_relay(True, zi, q).start()
+
+                @pl.when((zi > a) & (a > 0))
+                def _():
+                    tail_relay(False, zi, q).start()
+
+            return body
+
+        def run(q):
+            group(s, column(q))
+            group(s, tails(q))
+
+        return run
+
+    def pick(s):
+        def run(q):
+            @pl.when(q % 2 == 0)
+            def _():
+                def body(zi):
+                    named = jnp.concatenate(
+                        [unit_notes[zi, q, 0:1, :], unit_notes[zi, q + 1, 0:1, :]], axis=1
+                    )
+                    down = lax.broadcasted_iota(jnp.int32, (2 * pair, 2 * pair), 0)
+                    right = lax.broadcasted_iota(jnp.int32, (2 * pair, 2 * pair), 1)
+                    named = jnp.sum(
+                        jnp.where(down == right, named, 0.0), axis=1, keepdims=True
+                    )
+                    number = lax.broadcasted_iota(jnp.int32, (2 * pair, slots), 1).astype(f32)
+                    chosen[...] = jnp.where(number == named, 1.0, 0.0).astype(bf16)
+                    for t in range(0, width, tile):
+                        found = jnp.dot(
+                            chosen[...], cache[:, t:t + tile], preferred_element_type=f32
+                        ).astype(bf16)
+                        picked[zi, q, :, t:t + tile] = found[:pair]
+                        picked[zi, q + 1, :, t:t + tile] = found[pair:]
+
+                group(s, body)
+
+        return run
+
+    def multiply(s):
+        def run(q):
+            def body(zi):
+                head_copy(zi, q).wait_recv()
+                queries = qall[zi, q].reshape(pair, width)
+                lpart[q, zi, 0:columns, :] = lax.dot_general(
+                    p_ref[...], queries, over_width, preferred_element_type=f32
+                )
+                mixed = lax.dot_general(
+                    picked[zi, q], queries, over_width, preferred_element_type=f32
+                )
+                hard = jnp.sum(jnp.where(diagonal(), mixed, 0.0), axis=0, keepdims=True)
+                lpart[q, zi, columns:columns + 8, :] = jnp.broadcast_to(hard, (8, pair))
+
+                @pl.when(zi % 2 != core)
+                def _():
+                    core_copy(zi, q).start()
+
+            group(s, body)
+
+        return run
+
+    def add_core(s):
+        def run(q):
+            def body(zi):
+                core_copy(zi, q).wait_recv()
+                ypart[q, zi // 2, y] = lpart[q, zi] + cpart[q, zi // 2]
+                for k in range(1, n_line):
+                    line_copy(zi, q, k).start()
+
+            group(s, owned(body))
+
+        return run
+
+    def scored(zi, q, t):
+        values = scale * lpart[q, zi, t * BLOCK:(t + 1) * BLOCK, :]
+        block = sources_ref[me * parts + t].astype(f32)
+        query = (zi * 2 + right_half) * rows + q * part + lane - right_half * part
+        positive = (sub + (me * columns + t * BLOCK)) == query
+        allowed = (unit_notes[zi, q, 1:2, :] != block) | positive
+        return jnp.where(allowed, values, NEG_FILL), positive
+
+    def scored_hard(zi, q):
+        values = scale * lpart[q, zi, columns:columns + 1, :]
+        return jnp.where(unit_notes[zi, q, 0:1, :] >= 0.0, values, NEG_FILL)
+
+    def local_stats(s):
+        def run(q):
+            def body(zi):
+                for k in range(1, n_line):
+                    line_copy(zi, q, k).wait_recv()
+                total = ypart[q, zi // 2, 0]
+                for k in range(1, n_line):
+                    total = total + ypart[q, zi // 2, k]
+                lpart[q, zi] = total
+                hard = scored_hard(zi, q)
+                blocks = [scored(zi, q, t)[0] for t in range(parts)]
+                top = hard
+                for block in blocks:
+                    top = jnp.maximum(top, jnp.max(block, axis=0, keepdims=True))
+                added = jnp.exp(hard - top)
+                for block in blocks:
+                    added = added + jnp.sum(jnp.exp(block - top), axis=0, keepdims=True)
+                stat_own[q, 0, pl.ds(zi // 2, 1), :] = top
+                stat_own[q, 1, pl.ds(zi // 2, 1), :] = added
+
+            group(s, owned(body))
+            if s == far:
+                for j in range(1, n):
+                    stat_copy(j, q).start()
+                stat_all[q, me] = stat_own[q]
+
+        return run
+
+    def weigh(q):
+        for j in range(1, n):
+            stat_copy(j, q).wait_recv()
+        top = stat_all[q, 0, 0]
+        for j in range(1, n):
+            top = jnp.maximum(top, stat_all[q, j, 0])
+        total = stat_all[q, 0, 1] * jnp.exp(stat_all[q, 0, 0] - top)
+        for j in range(1, n):
+            total = total + stat_all[q, j, 1] * jnp.exp(stat_all[q, j, 0] - top)
+        peak[...] = top
+        mass[...] = total
+
+        def body(zi):
+            high = peak[pl.ds(zi // 2, 1), :]
+            whole = mass[pl.ds(zi // 2, 1), :]
+            own_logit = jnp.zeros((1, pair), f32)
+            for t in range(parts):
+                masked, positive = scored(zi, q, t)
+                weight = jnp.exp(masked - high) / whole - positive.astype(f32)
+                wts[q, zi, t * BLOCK:(t + 1) * BLOCK, :] = weight.astype(bf16)
+                own_logit = own_logit + jnp.sum(
+                    jnp.where(positive, masked, 0.0), axis=0, keepdims=True
+                )
+            hard = jnp.exp(scored_hard(zi, q) - high) / whole
+            wts[q, zi, columns:columns + 16, :] = jnp.broadcast_to(hard, (16, pair)).astype(bf16)
+            weight_copy(zi, q).start()
+            counted = ((zi * 2 + right_half) == me).astype(jnp.int32) > 0
+            lsum[...] += jnp.where(counted, high + jnp.log(whole) - own_logit, 0.0)
+
+        @pl.loop(0, lines)
+        def _(zi):
+            owned(body)(zi)
+
+    def send_across(q):
+        def body(zi):
+            @pl.when(zi % 2 != core)
+            def _():
+                weight_copy(zi, q).wait_recv()
+
+            hard = wts[q, zi, columns:columns + 1, :].astype(f32)
+            chooser = jnp.where(diagonal(), hard, 0.0).astype(bf16)
+            for t in range(0, width, tile):
+                out = lax.dot_general(
+                    wts[q, zi, 0:columns, :], p_ref[:, t:t + tile], over_rows,
+                    preferred_element_type=f32,
+                )
+                acc[q % 2, zi, :, t:t + tile] = out + jnp.dot(
+                    chooser, picked[zi, q, :, t:t + tile], preferred_element_type=f32
+                )
+            other = pl.ds(pl.multiple_of((1 - b) * part, part), direct)
+            xsend[q, zi] = acc[q % 2, zi, other, :].astype(bf16)
+            cross_copy(zi, q).start()
+
+        for s in range(far, -1, -1):
+            group(s, body)
+
+    mine = pl.ds(pl.multiple_of(b * part, part), part)
+    mine_head = pl.ds(pl.multiple_of(b * part, part), direct)
+    mine_tail = pl.ds(pl.multiple_of(b * part + direct, 16), rest)
+    other_tail = pl.ds(pl.multiple_of((1 - b) * part + direct, 16), rest)
+
+    def add_line(zi, q, slot):
+        acc[q % 2, zi, mine, :] += zrecv[q, slot, 0:part, :].astype(f32)
+        acc[q % 2, zi, other_tail, :] += zrecv[q, slot, part:part + rest, :].astype(f32)
+
+    def pass_on(s):
+        def run(q):
+            def body(zi):
+                cross_copy(zi, q).wait_recv()
+                acc[q % 2, zi, mine_head, :] += xrecv[q, zi].astype(f32)
+
+                @pl.when(((zi > a) & (a > 0)) | ((zi < a) & (a < far)))
+                def _():
+                    up_copy(zi, q).wait_recv()
+                    add_line(zi, q, zi)
+
+                zsend[q, zi, 0:part, :] = acc[q % 2, zi, mine, :].astype(bf16)
+                zsend[q, zi, part:part + rest, :] = acc[q % 2, zi, other_tail, :].astype(bf16)
+
+                @pl.when(zi > a)
+                def _():
+                    up_copy(zi, q).start()
+
+                @pl.when(zi < a)
+                def _():
+                    down_copy(zi, q, int(s == 1)).start()
+
+            group(s, body)
+
+        return run
+
+    def gather_own(q):
+        cross_copy(a, q).wait_recv()
+        acc[q % 2, a, mine_head, :] += xrecv[q, a].astype(f32)
+
+        @pl.when(a > 0)
+        def _():
+            up_copy(a, q).wait_recv()
+            add_line(a, q, a)
+
+        @pl.when(a < far)
+        def _():
+            down_copy(a, q, 1).wait_recv()
+            add_line(a, q, lines)
+
+        zsend[q, a, part:part + rest, :] = acc[q % 2, a, other_tail, :].astype(bf16)
+        rest_copy(q).start()
+
+    def finish(q):
+        rest_copy(q).wait_recv()
+        acc[q % 2, a, mine_tail, :] += lrest[q].astype(f32)
+        qgrad[pl.ds(pl.multiple_of(q * part, part), part), :] = acc[q % 2, a, mine, :].astype(bf16)
+
+    def passage_terms(q):
+        for t in range(0, width, tile):
+            total = pacc[:, t:t + tile]
+            for zi in range(lines):
+                total = total + jnp.dot(
+                    wts[q, zi, 0:columns, :],
+                    qall[zi, q, :, :, t:t + tile].reshape(pair, tile),
+                    preferred_element_type=f32,
+                )
+            pacc[:, t:t + tile] = total
+
+    def tell_loss(q):
+        @pl.when(q == stages - 1)
+        def _():
+            loss_own[...] = jnp.broadcast_to(lsum[...], (8, pair))
+            for j in range(1, n):
+                loss_copy(j).start()
+            loss_all[me] = loss_own[...]
+
+    start_own(0)
+    for j in range(1, n):
+        note_copy(j).start()
+    notes[me] = note_own[me]
+    for j in range(1, n):
+        note_copy(j).wait_recv()
+
+    @pl.loop(0, lines)
+    def _(zi):
+        for q in range(stages):
+            cut = slice(q * part, (q + 1) * part)
+            unit_notes[zi, q] = jnp.concatenate(
+                [notes[zi * 2, :, cut], notes[zi * 2 + 1, :, cut]], axis=1
+            )
+
+    load_cache.wait()
+    for copy in own_q:
+        copy.wait()
+
+    acts = [(1, turn)]
+    acts += [(s, relay(s)) for s in range(1, lines)]
+    acts += [(period, lambda q: pl.when(q < stages - 1)(lambda: start_own(q + 1)))]
+    acts += [(2 * far + 5 - s, pass_on(s)) for s in range(1, lines)]
+    acts += [(2 * far + 5, gather_own), (2 * far + 6, finish)]
+    acts += [(far + 4, weigh)]
+    acts += [(s + 3, local_stats(s)) for s in range(lines)]
+    acts += [(s + 2, add_core(s)) for s in range(lines)]
+    acts += [(max(s - 1, 0), pick(s)) for s in range(lines)]
+    acts += [(s + 1, multiply(s)) for s in range(lines)]
+    acts += [(far + 4, send_across), (far + 5, tell_loss), (far + 6, passage_terms)]
+    depth = max(o for o, _ in acts) // period
+
+    @pl.loop(0, stages + depth)
+    def _(turn_at):
+        for j in range(period):
+            for o, act in acts:
+                if o % period == j:
+                    q = turn_at - o // period
+
+                    @pl.when((q >= 0) & (q < stages))
+                    def _():
+                        act(q)
+
+    pgrad[...] = pacc[...].astype(bf16)
+    for j in range(1, n):
+        loss_copy(j).wait_recv()
+    sums = loss_all[0]
+    for j in range(1, n):
+        sums = sums + loss_all[j]
+    loss_mine[...] = sums
+    loss_core.start()
+    loss_core.wait_recv()
+    loss_out[...] = jnp.broadcast_to(
+        jnp.sum(loss_mine[...] + loss_beside[...], axis=1, keepdims=True), (8, pair)
+    )
+
+    def sent(zi, q):
+        @pl.when((zi <= a) & (a < far))
+        def _():
+            column_copy(True, zi, q).wait_send()
+            tail_relay(True, zi, q).wait_send()
+
+        @pl.when((zi >= a) & (a > 0))
+        def _():
+            column_copy(False, zi, q).wait_send()
+            tail_relay(False, zi, q).wait_send()
+
+        head_copy(zi, q).wait_send()
+        cross_copy(zi, q).wait_send()
+
+        @pl.when(zi != a)
+        def _():
+            up_copy(zi, q).wait_send()
+
+        @pl.when(zi % 2 != core)
+        def _():
+            core_copy(zi, q).wait_send()
+
+        @pl.when(zi % 2 == core)
+        def _():
+            weight_copy(zi, q).wait_send()
+            for k in range(1, n_line):
+                line_copy(zi, q, k).wait_send()
+
+    @pl.loop(0, stages)
+    def _(q):
+        @pl.loop(0, lines)
+        def _(zi):
+            sent(zi, q)
+
+        tail_copy(q).wait_send()
+        rest_copy(q).wait_send()
+        for j in range(1, n):
+            stat_copy(j, q).wait_send()
+
+    for j in range(1, n):
+        note_copy(j).wait_send()
+        loss_copy(j).wait_send()
+    loss_core.wait_send()
+
+
+def fused(queries, passages, cached, shard, row, source, block_source, n, n_row, scale):
+    rows, width = queries.shape
+    columns = passages.shape[0]
+    slots = cached.shape[0]
+    lines = n // 2
+    n_line = n_row // 2
+    pair = LANES
+    part = pair // 2
+    stages = rows // part
+    direct = part * 3 // 4
+    rest = part - direct
+    held = (lines + 1) // 2
+    f32 = jnp.float32
+    bf16 = jnp.bfloat16
+    vmem = pl.BlockSpec(memory_space=pltpu.VMEM)
+    mem = pltpu.VMEM
+    dma = pltpu.SemaphoreType.DMA
+    wires = max(n_line - 1, 1)
+    return pl.pallas_call(
+        functools.partial(fused_kernel, n, n_row, stages, direct, scale),
+        name="fused_loss",
+        out_shape=(
+            jax.ShapeDtypeStruct((rows, width), bf16),
+            jax.ShapeDtypeStruct((columns, width), bf16),
+            jax.ShapeDtypeStruct((8, pair), f32),
+        ),
+        in_specs=[
+            pl.BlockSpec(memory_space=pltpu.SMEM), vmem, vmem, vmem, vmem, vmem,
+            pl.BlockSpec(memory_space=pl.ANY),
+        ],
+        out_specs=(vmem, vmem, vmem),
+        scratch_shapes=[
+            mem((lines, stages, 2, part, width), bf16),
+            mem((slots, width), bf16),
+            mem((lines, stages, pair, width), bf16),
+            mem((2 * pair, slots), bf16),
+            mem((n, 2, rows), f32),
+            mem((n, 2, rows), f32),
+            mem((lines, stages, 2, pair), f32),
+            mem((stages, lines, columns + 8, pair), f32),
+            mem((stages, held, columns + 8, pair), f32),
+            mem((stages, held, n_line, columns + 8, pair), f32),
+            mem((held, pair), f32),
+            mem((held, pair), f32),
+            mem((stages, 2, held, pair), f32),
+            mem((stages, n, 2, held, pair), f32),
+            mem((stages, lines, columns + 16, pair), bf16),
+            mem((2, lines, pair, width), f32),
+            mem((columns, width), f32),
+            mem((stages, lines, direct, width), bf16),
+            mem((stages, lines, direct, width), bf16),
+            mem((stages, lines, part + rest, width), bf16),
+            mem((stages, lines + 1, part + rest, width), bf16),
+            mem((1, pair), f32),
+            mem((stages, rest, width), bf16),
+            mem((8, pair), f32),
+            mem((n, 8, pair), f32),
+            mem((8, pair), f32),
+            mem((8, pair), f32),
+            dma((6, lines, stages)), dma((3, lines, stages)),
+            dma((n - 1,)), dma((n - 1,)),
+            dma((stages, lines)), dma((stages, lines)),
+            dma((stages, lines, wires)), dma((stages, lines, wires)),
+            dma((stages, n - 1)), dma((stages, n - 1)),
+            dma((stages, lines)), dma((stages, lines)),
+            dma((stages, lines)), dma((stages, lines)),
+            dma((stages, lines)), dma((stages, lines + 1)),
+            dma((stages,)), dma((stages,)),
+            dma((n,)), dma((n,)),
+            dma((1 + stages,)),
+        ],
+        compiler_params=pltpu.CompilerParams(
+            collective_id=0, has_side_effects=True, vmem_limit_bytes=56 * 2**20
+        ),
+    )(block_source, shard, row, source, queries, passages, cached)
+
+
+def hand_out_kernel(share, q_ref, p_ref, loss_ref, q_out, p_out, loss_out, held, in_sem, out_sem):
+    chunks = in_sem.shape[1]
+    size = q_ref.shape[0] // chunks
+    pairs = ((q_ref, q_out), (p_ref, p_out))
+
+    def take(t, k):
+        at = pl.ds(k * size, size)
+        return pltpu.make_async_copy(pairs[t][0].at[at], held.at[t, at], in_sem.at[t, k])
+
+    def give(t, k):
+        at = pl.ds(k * size, size)
+        return pltpu.make_async_copy(held.at[t, at], pairs[t][1].at[at], out_sem.at[t, k])
+
+    for k in range(chunks):
+        for t in range(2):
+            take(t, k).start()
+    loss_out[0, 0] = share * jnp.sum(loss_ref[0:1, 0:1])
+    for k in range(chunks):
+        for t in range(2):
+            take(t, k).wait()
+            give(t, k).start()
+    for k in range(chunks):
+        for t in range(2):
+            give(t, k).wait()
+
+
+def hand_out(query_grad, passage_grad, losses, share):
+    rows, width = query_grad.shape
+    vmem = pl.BlockSpec(memory_space=pltpu.VMEM)
+    any_space = pl.BlockSpec(memory_space=pl.ANY)
+    dma = pltpu.SemaphoreType.DMA
+    chunks = 4
+    return pl.pallas_call(
+        functools.partial(hand_out_kernel, share),
+        name="hand_out",
+        out_shape=(
+            jax.ShapeDtypeStruct(query_grad.shape, query_grad.dtype),
+            jax.ShapeDtypeStruct(passage_grad.shape, passage_grad.dtype),
+            jax.ShapeDtypeStruct((1, 1), jnp.float32),
+        ),
+        in_specs=[any_space, any_space, vmem],
+        out_specs=(any_space, any_space, pl.BlockSpec(memory_space=pltpu.SMEM)),
+        scratch_shapes=[
+            pltpu.VMEM((2, rows, width), query_grad.dtype),
+            dma((2, chunks)), dma((2, chunks)),
+        ],
+    )(query_grad, passage_grad, losses)
+
+
+def on_device_fused(queries, passages, cached, hard_shard, hard_row, query_source, block_source):
+    n = lax.axis_size("dp")
+    n_row = lax.axis_size("row")
+    rows = queries.shape[0]
+    query_grad, passage_grad, losses = fused(
+        queries, passages, cached, hard_shard.T, hard_row.T, query_source.reshape(1, rows),
+        block_source, n, n_row, 1.0 / math.sqrt(D)
+    )
+    query_grad, passage_grad, loss = hand_out(
+        query_grad, passage_grad, losses, 1.0 / (rows * n)
+    )
+    return (loss.reshape(()), query_grad, passage_grad)
+
+
+def fits(n, n_row, rows, width, slots):
+    blocks = 2 * (n * rows * width * 2 + (2 * n + 2) * rows * width + slots * width)
+    half = rows // 2
+    scores = n * (3 + n_row // 2) * (rows + 8) * half * 4
+    return blocks + scores < 48 * 2**20
+
+
 def solution(mesh):
     in_specs = (
         P("dp", "row"),
@@ -596,6 +1319,14 @@
         P(),
     )
     out_specs = (P(), P("dp", "row"), P("dp", "row"))
+
+    def body(queries, passages, cached, *rest):
+        rows, width = queries.shape
+        n, n_row = mesh.shape["dp"], mesh.shape["row"]
+        if fits(n, n_row, rows, width, cached.shape[0]):
+            return on_device_fused(queries, passages, cached, *rest)
+        return on_device(queries, passages, cached, *rest)
+
     return jax.shard_map(
-        on_device, mesh=mesh, in_specs=in_specs, out_specs=out_specs, check_vma=False
+        body, mesh=mesh, in_specs=in_specs, out_specs=out_specs, check_vma=False
     )

time: 270 us -> 144 us (0.53)
  Pallas kernels: 191 us -> 143 us
  local copies, waits for them, and re-layouts: 32.5 us -> 0 us
  other arithmetic: 15.4 us -> 0 us
  blocking collectives: 13.6 us -> 0 us
  matrix products: 8.51 us -> 0 us
  starting transfers between devices: 4.45 us -> 0 us
  between operations: 3.38 us -> 0.64 us
    pallas_call x4 -> x2, Pallas kernels: 191 us -> 143 us  [the longest x1 140 us: fused(): pl.pallas_call(functools.partial(fused_kernel, n, n_row, stages, direct,...]
    gather x3 -> x0, local copies, waits for them, and re-layouts: 22.5 us -> none  [the longest x1 8.85 us: fetch_hard(): jnp.take(cached, asked_rows[:, common:].reshape(-1), axis=0, mode='clip')]
    all_to_all x1 -> x0, blocking collectives: 13.6 us -> none  [fetch_hard(): lax.all_to_all(requests, 'dp', split_axis=0, concat_axis=0, tiled=True)]
    dot_general x2 -> x0, matrix products: 8.51 us -> none  [the longest x1 4.74 us: on_device(): lax.dot_general(wcol.reshape(n_row, n_data, part, columns), qall.reshape(...]
    reduce_sum x7 -> x0, other arithmetic: 5.83 us -> none  [the longest x1 2.21 us: on_device(): jnp.sum(queries.astype(jnp.float32)[None] * hard_rows.astype(jnp.float32)...]
    all_to_all x1 -> x0, starting transfers between devices: 4.45 us -> none  [fetch_hard(): lax.all_to_all(picked, 'dp', split_axis=0, concat_axis=0, tiled=True)]
    scatter x1 -> x0, local copies, waits for them, and re-layouts: 4.32 us -> none  [fetch_hard(): jnp.zeros((n_data * capacity,), jnp.int32).at[target].set(wanted)]
    another operation x3 -> x0, other arithmetic: 3.08 us -> none
  transfers between devices with their start and end apart: 1 -> 0, of which waited for: 0 -> 0; matrix products, arithmetic and copies ran while one was open for 4% -> 0% of each run, Pallas kernels for 56% -> 0%
where the time goes in v2:
time: 144 us; the launch traced here: 143 us
  Pallas kernels  143 us (99%)
    pallas_call x1, Pallas kernels, fused(): pl.pallas_call(functools.partial(fused_kernel, n, n_row, stages, direct,...  140 us
    pallas_call x1, Pallas kernels, hand_out(): pl.pallas_call(functools.partial(hand_out_kernel, share), name='hand_out'...  3.27 us

profile of v2, /device:TPU:0, one launch (start us, length us, event | category | flops | bytes accessed | tf_op | source)
XLA Modules:
  0.0 143.4 jit_solution(1111979873024468753)
XLA Ops:
  0.6 139.5 %fused_loss.1 = (bf16[256,1024]{1,0:T(8,128)(2,1)}, bf16[256,1024]{1,0:T(8,128)(2,1)}, f32[8,128]{1,0:T(8,128)}) custom-call(s32[16]{0:T(128)} %sources_ref.1, s32[4,256]{1,0:T(4,128)} %bitcast.4, s32[4,256]{1,0:T(4,128)} %bitcast.5, s32[1,256]{1,0:T(1,128)} %bitcast.6, bf16[256,1024]{1,0:T(8,128)(2,1)} %q_ref.1, bf16[256,1024]{1,0:T(8,128)(2,1)} %p_ref.1, ...), custom_call_target="tpu_custom_call" | custom-call | tf_op jit(solution)/shard_map/fused_loss/pallas_call | solution.py:1182
  140.2 3.3 %hand_out.1 = (bf16[256,1024]{1,0:T(8,128)(2,1)}, bf16[256,1024]{1,0:T(8,128)(2,1)}, f32[1,1]{1,0:T(1,128)}) custom-call(bf16[256,1024]{1,0:T(8,128)(2,1)} %get-tuple-element.9.q_ref, bf16[256,1024]{1,0:T(8,128)(2,1)} %get-tuple-element.10.p_ref, f32[8,128]{1,0:T(8,128)} %get-tuple-element.11.loss_ref), custom_call_target="tpu_custom_call" | custom-call | tf_op jit(solution)/shard_map/hand_out/pallas_call | solution.py:1273

commit v3 on v2

--- a/solution.py
+++ b/solution.py
@@ -591,12 +591,11 @@
                  peak, mass, stat_own, stat_all, wts, acc, pacc, xsend, xrecv, zsend, zrecv,
                  lsum, lrest, loss_own, loss_all, loss_mine, loss_beside,
                  gsend, grecv, nsend, nrecv, csend, crecv, ysend, yrecv, ssend, srecv,
-                 wsend, wrecv, xs, xr, zs, zr, ms, mr, lsend, lrecv, own_sem):
+                 wsend, wrecv, xs, xr, zs, zr, ms, mr, lsend, lrecv, own_sem, qstage, pstage, out_sem):
     me = lax.axis_index("dp")
     r = lax.axis_index("row")
     lines = n // 2
     far = lines - 1
-    period = max(far, 1)
     a = me // 2
     b = me % 2
     n_line = n_row // 2
@@ -662,79 +661,105 @@
     def column_copy(up, zi, q, first=False):
         at = qall.at[zi, q, b]
         return remote(
-            own_rows(q, 0, part) if first else at, at, gsend.at[1 if up else 2, zi, q],
+            own_rows(q, 0, part) if first else at, at, gsend.at[1 if up else 2],
             grecv.at[0, zi, q], (me + 2 if up else me - 2, r),
         )
 
     def head_copy(zi, q, first=False):
         at = qall.at[zi, q, b, head]
         return remote(
-            own_rows(q, 0, direct) if first else at, at, gsend.at[0, zi, q],
+            own_rows(q, 0, direct) if first else at, at, gsend.at[0],
             grecv.at[1, zi, q], (across, r),
         )
 
     def tail_copy(q):
         return remote(
-            own_rows(q, direct, rest), qall.at[a, q, b, tail], gsend.at[3, a, q],
+            own_rows(q, direct, rest), qall.at[a, q, b, tail], gsend.at[3],
             grecv.at[2, a, q], (across, r),
         )
 
     def tail_relay(up, zi, q):
         at = qall.at[zi, q, 1 - b, tail]
         return remote(
-            at, at, gsend.at[4 if up else 5, zi, q], grecv.at[2, zi, q],
+            at, at, gsend.at[4 if up else 5], grecv.at[2, zi, q],
             (me + 2 if up else me - 2, r),
         )
 
     def note_copy(j):
         to = lax.rem(me + j, n)
         return remote(
-            note_own.at[to], notes.at[me], nsend.at[j - 1], nrecv.at[j - 1], (to, r)
+            note_own.at[to], notes.at[me], nsend.at[0], nrecv.at[0], (to, r)
         )
 
     def core_copy(zi, q):
         return remote(
-            lpart.at[q, zi], cpart.at[q, zi // 2], csend.at[q, zi], crecv.at[q, zi],
+            lpart.at[q, zi], cpart.at[q, zi // 2], csend.at[0], crecv.at[q, zi // 2],
             (me, partner),
         )
 
     def line_copy(zi, q, k):
         at = ypart.at[q, zi // 2, y]
         return remote(
-            at, at, ysend.at[q, zi, k - 1], yrecv.at[q, zi, k - 1],
+            at, at, ysend.at[0], yrecv.at[q, zi // 2],
             (me, lax.rem(r + 2 * k, n_row)),
         )
 
     def stat_copy(j, q):
         to = lax.rem(me + j, n)
         return remote(
-            stat_own.at[q], stat_all.at[q, me], ssend.at[q, j - 1], srecv.at[q, j - 1], (to, r)
+            stat_own.at[q], stat_all.at[q, me], ssend.at[0], srecv.at[q], (to, r)
         )
 
     def weight_copy(zi, q):
         at = wts.at[q, zi]
-        return remote(at, at, wsend.at[q, zi], wrecv.at[q, zi], (me, partner))
+        return remote(at, at, wsend.at[0], wrecv.at[q, zi // 2], (me, partner))
 
     def cross_copy(zi, q):
-        return remote(xsend.at[q, zi], xrecv.at[q, zi], xs.at[q, zi], xr.at[q, zi], (across, r))
-
-    def up_copy(zi, q):
-        return remote(zsend.at[q, zi], zrecv.at[q, zi], zs.at[q, zi], zr.at[q, zi], (me + 2, r))
-
-    def down_copy(zi, q, last):
-        slot = zi + last * (lines - zi)
+        return remote(xsend.at[q, zi], xrecv.at[q, zi], xs.at[0], xr.at[q, zi], (across, r))
+
+    between = lines > 2
+
+    def chains(zi):
+        if not between:
+            return zi < 0
+        return ((zi == 0) & (a == far - 1)) | ((zi == far) & (a == 1))
+
+    def line_out(zi, q, chained):
+        if chained:
+            toward = (zi == far).astype(jnp.int32) * 2 - 1
+            slot = lines + (zi == far).astype(jnp.int32)
+            to = a + toward
+        else:
+            slot = a
+            to = zi
         return remote(
-            zsend.at[q, zi], zrecv.at[q, slot], zs.at[q, zi], zr.at[q, slot], (me - 2, r)
+            zsend.at[q, zi], zrecv.at[q, slot], zs.at[0], zr.at[q, slot], (to * 2 + b, r)
+        )
+
+    def line_in(zi, q):
+        return remote(
+            zsend.at[q, zi], zrecv.at[q, zi], zs.at[0], zr.at[q, zi], (me, r)
+        )
+
+    def chain_in(zi, q):
+        slot = lines + (zi == far).astype(jnp.int32)
+        return remote(
+            zsend.at[q, zi], zrecv.at[q, slot], zs.at[0], zr.at[q, slot], (me, r)
         )
 
     def rest_copy(q):
-        return remote(zsend.at[q, a, pl.ds(part, rest)], lrest.at[q], ms.at[q], mr.at[q], (across, r))
+        return remote(zsend.at[q, a, pl.ds(part, rest)], lrest.at[q], ms.at[0], mr.at[q], (across, r))
 
     def loss_copy(j):
         to = lax.rem(me + j, n)
-        return remote(loss_own, loss_all.at[me], lsend.at[j - 1], lrecv.at[j - 1], (to, r))
-
-    loss_core = remote(loss_mine, loss_beside, lsend.at[n - 1], lrecv.at[n - 1], (me, partner))
+        return remote(loss_own, loss_all.at[me], lsend.at[0], lrecv.at[0], (to, r))
+
+    loss_core = remote(loss_mine, loss_beside, lsend.at[1], lrecv.at[1], (me, partner))
+
+    def whole(ref, send, recv):
+        return remote(ref, ref, send, recv, (me, r))
+
+    peers = pl.ds(0, n - 1)
 
     def group(s, body):
         if s == 0:
@@ -903,8 +928,9 @@
     def local_stats(s):
         def run(q):
             def body(zi):
-                for k in range(1, n_line):
-                    line_copy(zi, q, k).wait_recv()
+                if n_line > 1:
+                    at = ypart.at[q, zi // 2, pl.ds(0, n_line - 1)]
+                    whole(at, ysend.at[0], yrecv.at[q, zi // 2]).wait_recv()
                 total = ypart[q, zi // 2, 0]
                 for k in range(1, n_line):
                     total = total + ypart[q, zi // 2, k]
@@ -929,8 +955,7 @@
         return run
 
     def weigh(q):
-        for j in range(1, n):
-            stat_copy(j, q).wait_recv()
+        whole(stat_all.at[q, peers], ssend.at[0], srecv.at[q]).wait_recv()
         top = stat_all[q, 0, 0]
         for j in range(1, n):
             top = jnp.maximum(top, stat_all[q, j, 0])
@@ -974,11 +999,11 @@
                     wts[q, zi, 0:columns, :], p_ref[:, t:t + tile], over_rows,
                     preferred_element_type=f32,
                 )
-                acc[q % 2, zi, :, t:t + tile] = out + jnp.dot(
+                acc[q, zi, :, t:t + tile] = out + jnp.dot(
                     chooser, picked[zi, q, :, t:t + tile], preferred_element_type=f32
                 )
             other = pl.ds(pl.multiple_of((1 - b) * part, part), direct)
-            xsend[q, zi] = acc[q % 2, zi, other, :].astype(bf16)
+            xsend[q, zi] = acc[q, zi, other, :].astype(bf16)
             cross_copy(zi, q).start()
 
         for s in range(far, -1, -1):
@@ -990,30 +1015,23 @@
     other_tail = pl.ds(pl.multiple_of((1 - b) * part + direct, 16), rest)
 
     def add_line(zi, q, slot):
-        acc[q % 2, zi, mine, :] += zrecv[q, slot, 0:part, :].astype(f32)
-        acc[q % 2, zi, other_tail, :] += zrecv[q, slot, part:part + rest, :].astype(f32)
+        acc[q, zi, mine, :] += zrecv[q, slot, 0:part, :].astype(f32)
+        acc[q, zi, other_tail, :] += zrecv[q, slot, part:part + rest, :].astype(f32)
 
     def pass_on(s):
         def run(q):
             def body(zi):
                 cross_copy(zi, q).wait_recv()
-                acc[q % 2, zi, mine_head, :] += xrecv[q, zi].astype(f32)
-
-                @pl.when(((zi > a) & (a > 0)) | ((zi < a) & (a < far)))
+                acc[q, zi, mine_head, :] += xrecv[q, zi].astype(f32)
+
+                @pl.when(chains(zi))
                 def _():
-                    up_copy(zi, q).wait_recv()
-                    add_line(zi, q, zi)
-
-                zsend[q, zi, 0:part, :] = acc[q % 2, zi, mine, :].astype(bf16)
-                zsend[q, zi, part:part + rest, :] = acc[q % 2, zi, other_tail, :].astype(bf16)
-
-                @pl.when(zi > a)
-                def _():
-                    up_copy(zi, q).start()
-
-                @pl.when(zi < a)
-                def _():
-                    down_copy(zi, q, int(s == 1)).start()
+                    chain_in(zi, q).wait_recv()
+                    add_line(zi, q, lines + (zi == far).astype(jnp.int32))
+
+                zsend[q, zi, 0:part, :] = acc[q, zi, mine, :].astype(bf16)
+                zsend[q, zi, part:part + rest, :] = acc[q, zi, other_tail, :].astype(bf16)
+                line_out(zi, q, between and s == far).start()
 
             group(s, body)
 
@@ -1021,25 +1039,28 @@
 
     def gather_own(q):
         cross_copy(a, q).wait_recv()
-        acc[q % 2, a, mine_head, :] += xrecv[q, a].astype(f32)
-
-        @pl.when(a > 0)
-        def _():
-            up_copy(a, q).wait_recv()
-            add_line(a, q, a)
-
-        @pl.when(a < far)
-        def _():
-            down_copy(a, q, 1).wait_recv()
-            add_line(a, q, lines)
-
-        zsend[q, a, part:part + rest, :] = acc[q % 2, a, other_tail, :].astype(bf16)
+        acc[q, a, mine_head, :] += xrecv[q, a].astype(f32)
+
+        def body(zi):
+            line_in(zi, q).wait_recv()
+            add_line(a, q, zi)
+
+        for s in range(far - 1 if between else far, 0, -1):
+            group(s, body)
+        zsend[q, a, part:part + rest, :] = acc[q, a, other_tail, :].astype(bf16)
         rest_copy(q).start()
+
+    def give_queries(q):
+        at = pl.ds(pl.multiple_of(q * part, part), part)
+        return pltpu.make_async_copy(qstage.at[at], qgrad.at[at], out_sem.at[q])
+
+    give_passages = pltpu.make_async_copy(pstage, pgrad, out_sem.at[stages])
 
     def finish(q):
         rest_copy(q).wait_recv()
-        acc[q % 2, a, mine_tail, :] += lrest[q].astype(f32)
-        qgrad[pl.ds(pl.multiple_of(q * part, part), part), :] = acc[q % 2, a, mine, :].astype(bf16)
+        acc[q, a, mine_tail, :] += lrest[q].astype(f32)
+        qstage[pl.ds(pl.multiple_of(q * part, part), part), :] = acc[q, a, mine, :].astype(bf16)
+        give_queries(q).start()
 
     def passage_terms(q):
         for t in range(0, width, tile):
@@ -1052,6 +1073,11 @@
                 )
             pacc[:, t:t + tile] = total
 
+        @pl.when(q == stages - 1)
+        def _():
+            pstage[...] = pacc[...].astype(bf16)
+            give_passages.start()
+
     def tell_loss(q):
         @pl.when(q == stages - 1)
         def _():
@@ -1060,52 +1086,57 @@
                 loss_copy(j).start()
             loss_all[me] = loss_own[...]
 
-    start_own(0)
     for j in range(1, n):
         note_copy(j).start()
-    notes[me] = note_own[me]
-    for j in range(1, n):
-        note_copy(j).wait_recv()
-
-    @pl.loop(0, lines)
-    def _(zi):
-        for q in range(stages):
-            cut = slice(q * part, (q + 1) * part)
-            unit_notes[zi, q] = jnp.concatenate(
-                [notes[zi * 2, :, cut], notes[zi * 2 + 1, :, cut]], axis=1
-            )
-
-    load_cache.wait()
-    for copy in own_q:
-        copy.wait()
-
-    acts = [(1, turn)]
-    acts += [(s, relay(s)) for s in range(1, lines)]
-    acts += [(period, lambda q: pl.when(q < stages - 1)(lambda: start_own(q + 1)))]
-    acts += [(2 * far + 5 - s, pass_on(s)) for s in range(1, lines)]
-    acts += [(2 * far + 5, gather_own), (2 * far + 6, finish)]
-    acts += [(far + 4, weigh)]
-    acts += [(s + 3, local_stats(s)) for s in range(lines)]
-    acts += [(s + 2, add_core(s)) for s in range(lines)]
-    acts += [(max(s - 1, 0), pick(s)) for s in range(lines)]
-    acts += [(s + 1, multiply(s)) for s in range(lines)]
-    acts += [(far + 4, send_across), (far + 5, tell_loss), (far + 6, passage_terms)]
-    depth = max(o for o, _ in acts) // period
-
-    @pl.loop(0, stages + depth)
-    def _(turn_at):
-        for j in range(period):
-            for o, act in acts:
-                if o % period == j:
-                    q = turn_at - o // period
-
-                    @pl.when((q >= 0) & (q < stages))
-                    def _():
-                        act(q)
-
-    pgrad[...] = pacc[...].astype(bf16)
-    for j in range(1, n):
-        loss_copy(j).wait_recv()
+    start_own(0)
+
+    def read_all(q):
+        read_notes()
+
+    def read_notes():
+        notes[me] = note_own[me]
+        whole(notes.at[peers], nsend.at[0], nrecv.at[0]).wait_recv()
+
+        @pl.loop(0, lines)
+        def _(zi):
+            for q in range(stages):
+                cut = slice(q * part, (q + 1) * part)
+                unit_notes[zi, q] = jnp.concatenate(
+                    [notes[zi * 2, :, cut], notes[zi * 2 + 1, :, cut]], axis=1
+                )
+
+        load_cache.wait()
+        for copy in own_q:
+            copy.wait()
+
+    begins = [0, 2, 4, 6]
+    weighs = [7, 9, 11, 13]
+    acts = []
+    acts += [([x + s + 3 for x in begins], local_stats(s)) for s in range(far, -1, -1)]
+    acts += [([x + s + 2 for x in begins], add_core(s)) for s in range(far, -1, -1)]
+    acts += [([x + 1 for x in begins], turn)]
+    acts += [([x + s for x in begins], relay(s)) for s in range(1, lines)]
+    acts += [([-1] + [x - 1 for x in begins[1:]], start_own)]
+    acts += [([x + 1 + (between and s == far - 1) for x in weighs], pass_on(s)) for s in range(far, 0, -1)]
+    acts += [(weighs, weigh)]
+    acts += [([1], read_all)]
+    acts += [([x + max(s, 1) for x in begins], pick(s)) for s in range(lines)]
+    acts += [([x + s + 1 for x in begins], multiply(s)) for s in range(lines)]
+    acts += [([x + 0 for x in weighs], send_across), ([x + 0 + 1 for x in weighs], tell_loss), ([x + 0 + 2 for x in weighs], passage_terms)]
+    acts += [([x + 3 for x in weighs], gather_own), ([x + 4 for x in weighs], finish)]
+    slots_in_all = max(max(times) for times, _ in acts) + 1
+
+    @pl.loop(0, slots_in_all)
+    def _(now):
+        for times, act in acts:
+            q = sum(i * (now == at).astype(jnp.int32) for i, at in enumerate(times))
+            due = sum((now == at).astype(jnp.int32) for at in times)
+
+            @pl.when(due > 0)
+            def _():
+                act(q)
+
+    whole(loss_all.at[peers], lsend.at[0], lrecv.at[0]).wait_recv()
     sums = loss_all[0]
     for j in range(1, n):
         sums = sums + loss_all[j]
@@ -1116,49 +1147,42 @@
         jnp.sum(loss_mine[...] + loss_beside[...], axis=1, keepdims=True), (8, pair)
     )
 
-    def sent(zi, q):
-        @pl.when((zi <= a) & (a < far))
-        def _():
-            column_copy(True, zi, q).wait_send()
-            tail_relay(True, zi, q).wait_send()
-
-        @pl.when((zi >= a) & (a > 0))
-        def _():
-            column_copy(False, zi, q).wait_send()
-            tail_relay(False, zi, q).wait_send()
-
-        head_copy(zi, q).wait_send()
-        cross_copy(zi, q).wait_send()
-
-        @pl.when(zi != a)
-        def _():
-            up_copy(zi, q).wait_send()
-
-        @pl.when(zi % 2 != core)
-        def _():
-            core_copy(zi, q).wait_send()
-
-        @pl.when(zi % 2 == core)
-        def _():
-            weight_copy(zi, q).wait_send()
-            for k in range(1, n_line):
-                line_copy(zi, q, k).wait_send()
-
-    @pl.loop(0, stages)
-    def _(q):
-        @pl.loop(0, lines)
-        def _(zi):
-            sent(zi, q)
-
-        tail_copy(q).wait_send()
-        rest_copy(q).wait_send()
-        for j in range(1, n):
-            stat_copy(j, q).wait_send()
-
-    for j in range(1, n):
-        note_copy(j).wait_send()
-        loss_copy(j).wait_send()
+    for at in range(lines):
+        up = pl.ds(0, at + 1)
+        down = pl.ds(0, lines - at)
+
+        @pl.when((a == at) & (a < far))
+        def _():
+            whole(qall.at[up, :, 0], gsend.at[1], grecv.at[0, 0, 0]).wait_send()
+            whole(qall.at[up, :, 0, pl.ds(0, rest)], gsend.at[4], grecv.at[0, 0, 0]).wait_send()
+
+        @pl.when((a == at) & (a > 0))
+        def _():
+            whole(qall.at[down, :, 0], gsend.at[2], grecv.at[0, 0, 0]).wait_send()
+            whole(qall.at[down, :, 0, pl.ds(0, rest)], gsend.at[5], grecv.at[0, 0, 0]).wait_send()
+
+    held = cpart.shape[1]
+    for ref, send, recv in (
+        (xsend, gsend.at[0], xr.at[0, 0]),
+        (lrest, gsend.at[3], mr.at[0]),
+        (notes.at[peers], nsend.at[0], nrecv.at[0]),
+        (cpart, csend.at[0], crecv.at[0, 0]),
+        (stat_all.at[:, peers], ssend.at[0], srecv.at[0]),
+        (wts.at[:, pl.ds(0, held)], wsend.at[0], wrecv.at[0, 0]),
+        (xsend, xs.at[0], xr.at[0, 0]),
+        (lrest, ms.at[0], mr.at[0]),
+        (loss_all.at[peers], lsend.at[0], lrecv.at[0]),
+    ):
+        whole(ref, send, recv).wait_send()
+    if far > 0:
+        whole(zsend.at[:, pl.ds(0, far)], zs.at[0], zr.at[0, 0]).wait_send()
+    if n_line > 1:
+        sent = ypart.at[:, :, pl.ds(0, n_line - 1)]
+        whole(sent, ysend.at[0], yrecv.at[0, 0]).wait_send()
     loss_core.wait_send()
+    for q in range(stages):
+        give_queries(q).wait()
+    give_passages.wait()
 
 
 def fused(queries, passages, cached, shard, row, source, block_source, n, n_row, scale):
@@ -1178,7 +1202,6 @@
     vmem = pl.BlockSpec(memory_space=pltpu.VMEM)
     mem = pltpu.VMEM
     dma = pltpu.SemaphoreType.DMA
-    wires = max(n_line - 1, 1)
     return pl.pallas_call(
         functools.partial(fused_kernel, n, n_row, stages, direct, scale),
         name="fused_loss",
@@ -1191,7 +1214,9 @@
             pl.BlockSpec(memory_space=pltpu.SMEM), vmem, vmem, vmem, vmem, vmem,
             pl.BlockSpec(memory_space=pl.ANY),
         ],
-        out_specs=(vmem, vmem, vmem),
+        out_specs=(
+            pl.BlockSpec(memory_space=pl.ANY), pl.BlockSpec(memory_space=pl.ANY), vmem
+        ),
         scratch_shapes=[
             mem((lines, stages, 2, part, width), bf16),
             mem((slots, width), bf16),
@@ -1208,28 +1233,31 @@
             mem((stages, 2, held, pair), f32),
             mem((stages, n, 2, held, pair), f32),
             mem((stages, lines, columns + 16, pair), bf16),
-            mem((2, lines, pair, width), f32),
+            mem((stages, lines, pair, width), f32),
             mem((columns, width), f32),
             mem((stages, lines, direct, width), bf16),
             mem((stages, lines, direct, width), bf16),
             mem((stages, lines, part + rest, width), bf16),
-            mem((stages, lines + 1, part + rest, width), bf16),
+            mem((stages, lines + 2, part + rest, width), bf16),
             mem((1, pair), f32),
             mem((stages, rest, width), bf16),
             mem((8, pair), f32),
             mem((n, 8, pair), f32),
             mem((8, pair), f32),
             mem((8, pair), f32),
-            dma((6, lines, stages)), dma((3, lines, stages)),
-            dma((n - 1,)), dma((n - 1,)),
-            dma((stages, lines)), dma((stages, lines)),
-            dma((stages, lines, wires)), dma((stages, lines, wires)),
-            dma((stages, n - 1)), dma((stages, n - 1)),
-            dma((stages, lines)), dma((stages, lines)),
-            dma((stages, lines)), dma((stages, lines)),
-            dma((stages, lines)), dma((stages, lines + 1)),
-            dma((stages,)), dma((stages,)),
-            dma((n,)), dma((n,)),
+            dma((6,)), dma((3, lines, stages)),
+            dma((1,)), dma((1,)),
+            dma((1,)), dma((stages, held)),
+            dma((1,)), dma((stages, held)),
+            dma((1,)), dma((stages,)),
+            dma((1,)), dma((stages, held)),
+            dma((1,)), dma((stages, lines)),
+            dma((1,)), dma((stages, lines + 2)),
+            dma((1,)), dma((stages,)),
+            dma((2,)), dma((2,)),
+            dma((1 + stages,)),
+            mem((rows, width), bf16),
+            mem((columns, width), bf16),
             dma((1 + stages,)),
         ],
         compiler_params=pltpu.CompilerParams(
@@ -1305,7 +1333,7 @@
     blocks = 2 * (n * rows * width * 2 + (2 * n + 2) * rows * width + slots * width)
     half = rows // 2
     scores = n * (3 + n_row // 2) * (rows + 8) * half * 4
-    return blocks + scores < 48 * 2**20
+    return blocks + scores < 48 * 2**20 and n % 4 == 0
 
 
 def solution(mesh):

time: 144 us -> 120 us (0.83)
  Pallas kernels: 143 us -> 119 us
    pallas_call x1, Pallas kernels: 140 us -> 116 us  [fused(): pl.pallas_call(functools.partial(fused_kernel, n, n_row, stages, direct,...]
where the time goes in v3:
time: 120 us
  Pallas kernels  119 us (99%)
    pallas_call x1, Pallas kernels, fused(): pl.pallas_call(functools.partial(fused_kernel, n, n_row, stages, direct,...  116 us
    pallas_call x1, Pallas kernels, hand_out(): pl.pallas_call(functools.partial(hand_out_kernel, share), name='hand_out'...  3.27 us

profile of v3, /device:TPU:0, one launch (start us, length us, event | category | flops | bytes accessed | tf_op | source)
XLA Modules:
  0.0 119.7 jit_solution(807271474103693300)
XLA Ops:
  0.6 115.8 %fused_loss.1 = (bf16[256,1024]{1,0:T(8,128)(2,1)}, bf16[256,1024]{1,0:T(8,128)(2,1)}, f32[8,128]{1,0:T(8,128)}) custom-call(s32[16]{0:T(128)} %sources_ref.1, s32[4,256]{1,0:T(4,128)} %bitcast.4, s32[4,256]{1,0:T(4,128)} %bitcast.5, s32[1,256]{1,0:T(1,128)} %bitcast.6, bf16[256,1024]{1,0:T(8,128)(2,1)} %q_ref.1, bf16[256,1024]{1,0:T(8,128)(2,1)} %p_ref.1, ...), custom_call_target="tpu_custom_call" | custom-call | tf_op jit(solution)/shard_map/fused_loss/pallas_call | solution.py:1205
  116.4 3.3 %hand_out.1 = (bf16[256,1024]{1,0:T(8,128)(2,1)}, bf16[256,1024]{1,0:T(8,128)(2,1)}, f32[1,1]{1,0:T(1,128)}) custom-call(bf16[256,1024]{1,0:T(8,128)(2,1)} %get-tuple-element.9.q_ref, bf16[256,1024]{1,0:T(8,128)(2,1)} %get-tuple-element.10.p_ref, f32[8,128]{1,0:T(8,128)} %get-tuple-element.11.loss_ref), custom_call_target="tpu_custom_call" | custom-call | tf_op jit(solution)/shard_map/hand_out/pallas_call | solution.py:1301

commit v4 on v3

--- a/solution.py
+++ b/solution.py
@@ -1109,21 +1109,32 @@
         for copy in own_q:
             copy.wait()
 
-    begins = [0, 2, 4, 6]
-    weighs = [7, 9, 11, 13]
-    acts = []
-    acts += [([x + s + 3 for x in begins], local_stats(s)) for s in range(far, -1, -1)]
-    acts += [([x + s + 2 for x in begins], add_core(s)) for s in range(far, -1, -1)]
-    acts += [([x + 1 for x in begins], turn)]
-    acts += [([x + s for x in begins], relay(s)) for s in range(1, lines)]
-    acts += [([-1] + [x - 1 for x in begins[1:]], start_own)]
-    acts += [([x + 1 + (between and s == far - 1) for x in weighs], pass_on(s)) for s in range(far, 0, -1)]
-    acts += [(weighs, weigh)]
-    acts += [([1], read_all)]
-    acts += [([x + max(s, 1) for x in begins], pick(s)) for s in range(lines)]
-    acts += [([x + s + 1 for x in begins], multiply(s)) for s in range(lines)]
-    acts += [([x + 0 for x in weighs], send_across), ([x + 0 + 1 for x in weighs], tell_loss), ([x + 0 + 2 for x in weighs], passage_terms)]
-    acts += [([x + 3 for x in weighs], gather_own), ([x + 4 for x in weighs], finish)]
+    begins = [lines * q for q in range(stages)]
+    weighs = [x + 2 * far + 4 for x in begins]
+    falling = range(far, -1, -1)
+    multiplied = [2 * s + 1 - (s == far) for s in range(lines)]
+    counted = [min(x + 3, 2 * far + 2) for x in multiplied]
+
+    def at(first, shift):
+        return [x + shift for x in first]
+
+    acts = [(at(begins, counted[s]), local_stats(s)) for s in falling if counted[s] < 2 * far + 2]
+    acts += [(at(begins, multiplied[s] + 1), add_core(s)) for s in falling]
+    acts += [(at(begins, 2 * s - 1), relay(s)) for s in range(far, 1, -1)]
+    acts += [(at(begins, 1), turn), (at(begins, 1), relay(1))]
+    acts += [([-1] + at(begins[1:], -2), start_own)]
+    acts += [
+        (at(weighs, 2 if s == far else 4 if s == far - 1 else 3), pass_on(s))
+        for s in range(far, 0, -1)
+    ]
+    acts += [(weighs, weigh), ([1], read_all)]
+    acts += [(at(begins, max(2 * s - (s == far), 1)), pick(s)) for s in range(lines)]
+    acts += [(at(begins, multiplied[s]), multiply(s)) for s in range(lines)]
+    acts += [
+        (at(begins, counted[s]), local_stats(s)) for s in range(lines) if counted[s] == 2 * far + 2
+    ]
+    acts += [(weighs, send_across), (at(weighs, 1), tell_loss), (at(weighs, 2), passage_terms)]
+    acts += [(at(weighs, 6), gather_own), (at(weighs, 8), finish)]
     slots_in_all = max(max(times) for times, _ in acts) + 1
 
     @pl.loop(0, slots_in_all)
@@ -1143,9 +1154,8 @@
     loss_mine[...] = sums
     loss_core.start()
     loss_core.wait_recv()
-    loss_out[...] = jnp.broadcast_to(
-        jnp.sum(loss_mine[...] + loss_beside[...], axis=1, keepdims=True), (8, pair)
-    )
+    both = loss_mine[0:1, :] + loss_beside[0:1, :]
+    loss_out[...] = jnp.sum(both, axis=1, keepdims=True) * (1.0 / (rows * n))
 
     for at in range(lines):
         up = pl.ds(0, at + 1)
@@ -1208,7 +1218,7 @@
         out_shape=(
             jax.ShapeDtypeStruct((rows, width), bf16),
             jax.ShapeDtypeStruct((columns, width), bf16),
-            jax.ShapeDtypeStruct((8, pair), f32),
+            jax.ShapeDtypeStruct((1, 1), f32),
         ),
         in_specs=[
             pl.BlockSpec(memory_space=pltpu.SMEM), vmem, vmem, vmem, vmem, vmem,
@@ -1266,8 +1276,8 @@
     )(block_source, shard, row, source, queries, passages, cached)
 
 
-def hand_out_kernel(share, q_ref, p_ref, loss_ref, q_out, p_out, loss_out, held, in_sem, out_sem):
-    chunks = in_sem.shape[1]
+def hand_out_kernel(q_ref, p_ref, loss_ref, q_out, p_out, loss_out, held, loss, in_sem, out_sem):
+    chunks = in_sem.shape[1] - 1
     size = q_ref.shape[0] // chunks
     pairs = ((q_ref, q_out), (p_ref, p_out))
 
@@ -1279,10 +1289,14 @@
         at = pl.ds(k * size, size)
         return pltpu.make_async_copy(held.at[t, at], pairs[t][1].at[at], out_sem.at[t, k])
 
+    take_loss = pltpu.make_async_copy(loss_ref, loss, in_sem.at[0, chunks])
+    give_loss = pltpu.make_async_copy(loss, loss_out, out_sem.at[0, chunks])
+    take_loss.start()
     for k in range(chunks):
         for t in range(2):
             take(t, k).start()
-    loss_out[0, 0] = share * jnp.sum(loss_ref[0:1, 0:1])
+    take_loss.wait()
+    give_loss.start()
     for k in range(chunks):
         for t in range(2):
             take(t, k).wait()
@@ -1290,27 +1304,28 @@
     for k in range(chunks):
         for t in range(2):
             give(t, k).wait()
-
-
-def hand_out(query_grad, passage_grad, losses, share):
+    give_loss.wait()
+
+
+def hand_out(query_grad, passage_grad, losses):
     rows, width = query_grad.shape
-    vmem = pl.BlockSpec(memory_space=pltpu.VMEM)
     any_space = pl.BlockSpec(memory_space=pl.ANY)
     dma = pltpu.SemaphoreType.DMA
     chunks = 4
     return pl.pallas_call(
-        functools.partial(hand_out_kernel, share),
+        hand_out_kernel,
         name="hand_out",
         out_shape=(
             jax.ShapeDtypeStruct(query_grad.shape, query_grad.dtype),
             jax.ShapeDtypeStruct(passage_grad.shape, passage_grad.dtype),
             jax.ShapeDtypeStruct((1, 1), jnp.float32),
         ),
-        in_specs=[any_space, any_space, vmem],
-        out_specs=(any_space, any_space, pl.BlockSpec(memory_space=pltpu.SMEM)),
+        in_specs=[any_space, any_space, any_space],
+        out_specs=(any_space, any_space, any_space),
         scratch_shapes=[
             pltpu.VMEM((2, rows, width), query_grad.dtype),
-            dma((2, chunks)), dma((2, chunks)),
+            pltpu.VMEM((1, 1), jnp.float32),
+            dma((2, chunks + 1)), dma((2, chunks + 1)),
         ],
     )(query_grad, passage_grad, losses)
 
@@ -1323,9 +1338,7 @@
         queries, passages, cached, hard_shard.T, hard_row.T, query_source.reshape(1, rows),
         block_source, n, n_row, 1.0 / math.sqrt(D)
     )
-    query_grad, passage_grad, loss = hand_out(
-        query_grad, passage_grad, losses, 1.0 / (rows * n)
-    )
+    query_grad, passage_grad, loss = hand_out(query_grad, passage_grad, losses)
     return (loss.reshape(()), query_grad, passage_grad)
 
 

time: 120 us -> 117 us (0.975)
  Pallas kernels: 119 us -> 116 us
    pallas_call x1, Pallas kernels: 116 us -> 113 us  [fused(): pl.pallas_call(functools.partial(fused_kernel, n, n_row, stages, direct,...]
where the time goes in v4:
time: 117 us
  Pallas kernels  116 us (99%)
    pallas_call x1, Pallas kernels, fused(): pl.pallas_call(functools.partial(fused_kernel, n, n_row, stages, direct,...  113 us
    pallas_call x1, Pallas kernels, hand_out(): pl.pallas_call(hand_out_kernel, name='hand_out', out_shape=(jax.ShapeDtyp...  2.76 us

profile of v4, /device:TPU:0, one launch (start us, length us, event | category | flops | bytes accessed | tf_op | source)
XLA Modules:
  0.0 116.8 jit_solution(6116430713748168298)
XLA Ops:
  0.6 113.4 %fused_loss.1 = (bf16[256,1024]{1,0:T(8,128)(2,1)}, bf16[256,1024]{1,0:T(8,128)(2,1)}, f32[1,1]{1,0:T(1,128)}) custom-call(s32[16]{0:T(128)} %sources_ref.1, s32[4,256]{1,0:T(4,128)} %bitcast.4, s32[4,256]{1,0:T(4,128)} %bitcast.5, s32[1,256]{1,0:T(1,128)} %bitcast.6, bf16[256,1024]{1,0:T(8,128)(2,1)} %q_ref.1, bf16[256,1024]{1,0:T(8,128)(2,1)} %p_ref.1, ...), custom_call_target="tpu_custom_call" | custom-call | tf_op jit(solution)/shard_map/fused_loss/pallas_call | solution.py:1215
  114.0 2.8 %hand_out.1 = (bf16[256,1024]{1,0:T(8,128)(2,1)}, bf16[256,1024]{1,0:T(8,128)(2,1)}, f32[1,1]{1,0:T(1,128)}) custom-call(bf16[256,1024]{1,0:T(8,128)(2,1)} %get-tuple-element.9.q_ref, bf16[256,1024]{1,0:T(8,128)(2,1)} %get-tuple-element.10.p_ref, f32[1,1]{1,0:T(1,128)} %get-tuple-element.11.loss_ref), custom_call_target="tpu_custom_call" | custom-call | tf_op jit(solution)/shard_map/hand_out/pallas_call | solution.py:1315
